TPU v7x, 32 devices: a whole 2x2x4 slice. The times are simulated.
32 devices in a mesh: dp: 8 (over z, y), fsdp: 4 (over x, core).
Axes of the slice: x: 2, y: 2, z: 4, core: 2. Of those that a mesh axis runs over, the one named last changes fastest.
Arguments:
- tokens: bfloat16 [3, 4, 2048, 768], P(None, 'fsdp', 'dp'), may hold values from -6 to 6
- seq_lengths: int32 [3, 4, 2], P(None, 'fsdp'), may hold values from 1 to 1920, as said below
- norm_gain: bfloat16 [768], P('fsdp'), may hold values from 0.25 to 1.75
- w_inner: bfloat16 [768, 3072], P('fsdp'), may hold values from -0.21875 to 0.21875
- w_state: bfloat16 [768, 128], P('fsdp'), may hold values from -0.078125 to 0.078125
- w_step: bfloat16 [768, 48], P('fsdp'), may hold values from -0.21875 to 0.21875
- conv_weight: bfloat16 [4, 1664], P(None, 'fsdp'), may hold values from -3 to 3
- conv_bias: bfloat16 [1664], P('fsdp'), may hold values from -3 to 3
- step_bias: bfloat16 [48], P('fsdp'), may hold values from -2 to 1
- decay_log: bfloat16 [24], P('fsdp'), may hold values from -9.1875 to -2.296875
- skip_gain: bfloat16 [24], P('fsdp'), may hold values from 0.5 to 2
- out_gain: bfloat16 [1536], P('fsdp'), may hold values from 0.25 to 1.75
- w_out: bfloat16 [1536, 768], P('fsdp'), may hold values from -0.15625 to 0.15625
- cotangent: bfloat16 [3, 4, 2048, 768], P(None, 'fsdp', 'dp'), may hold values from -6 to 6
Outputs:
- layer_out: bfloat16 [3, 4, 2048, 768], P(None, 'fsdp', 'dp')
- tokens_grad: float32 [3, 4, 2048, 768], P(None, 'fsdp', 'dp')
- norm_gain_grad: float32 [768], P('fsdp')
- w_inner_grad: float32 [768, 3072], P('fsdp')
- w_state_grad: float32 [768, 128], P('fsdp')
- w_step_grad: float32 [768, 48], P('fsdp')
- conv_weight_grad: float32 [4, 1664], P(None, 'fsdp')
- conv_bias_grad: float32 [1664], P('fsdp')
- step_bias_grad: float32 [48], P('fsdp')
- decay_log_grad: float32 [24], P('fsdp')
- skip_gain_grad: float32 [24], P('fsdp')
- out_gain_grad: float32 [1536], P('fsdp')
- w_out_grad: float32 [1536, 768], P('fsdp')
Inputs may be any that keep to these rules, and one draw needn't show every extreme that they name: Each row of seq_lengths describes one span of 2048 positions: the first sequence begins at 0, the second at the first multiple of 128 at or after the first one's end, and it ends at or before 2048. For each group, in the span of one of the 3 micro-batches, one of the two sequences begins among the first 256 positions and ends among the last 256; in every other span both sequences have 2048 // 4 tokens or more. Some sequence has exactly 1920 tokens.
All inputs are finite; a program needn't handle non-finite values.
Results may differ from a plain program's by a relative error of at most 0.0045.
The roundings to bfloat16 on the way count: a program that leaves them out, or rounds other values in their place, can miss the bound.
Values may be sent and summed in bfloat16 or wider, within the bound.
A program may use at most 576 MiB of HBM per device.

v0:
```python
from functools import partial

import jax
import jax.numpy as jnp
from jax import lax
from jax.experimental import pallas as pl
from jax.experimental.pallas import tpu as pltpu
from jax.sharding import PartitionSpec as P

D = 768
INNER = 1536
HEADS = 24
HEAD_DIM = 64
STATE = 64
CONV = 4
BLOCK = 128
MB = 3
TOK_DEV = 256
HALO = 8
LANES = 128
CONV_COLS = INNER + 2 * STATE
WIDE = 2 * INNER + 2 * LANES
LATE = INNER + 2 * LANES
PAIRS = HEADS // 2
PARTS = 4
CHUNKS = MB * PARTS
LAG = 2
TURNS = 3
TURN_PAIRS = PAIRS // TURNS
CUTS = 3
EPSILON = 1e-05
HIGHEST = lax.Precision.HIGHEST
F32 = jnp.float32
BF16 = jnp.bfloat16
SENT = F32
ROWS = ((0,), (0,))
COLS = ((1,), (1,))
INNER_DIMS = ((1,), (0,))
VMEM_LIMIT = 60 * 1024 * 1024
SCALARS = pl.BlockSpec(memory_space=pltpu.SMEM)


def dot(left, right, dims=INNER_DIMS, precision=None):
    return lax.dot_general(left, right, (dims, ((), ())), precision=precision, preferred_element_type=F32)


def halves(value):
    high = value.astype(BF16)
    return high, (value - high.astype(F32)).astype(BF16)


def spread_operand(value):
    high, low = halves(value)
    return jnp.concatenate([high, low], axis=1)


def by_lane(first, second):
    low = iota(first.shape, 1) < STATE
    twice = jnp.where(low, first, second)
    high = twice.astype(BF16).astype(F32)
    return jnp.where(low, high, twice - high)


def twice(value, axis):
    return jnp.concatenate([value, value], axis=axis)


def fold(value):
    return value[:STATE] + value[STATE:]


def head_sums(value, selector):
    high, low = halves(value)
    return dot(high, selector) + dot(low, selector)


def sigmoid(value):
    return 1.0 / (1.0 + jnp.exp(-value))


def softplus(value):
    tail = jnp.exp(-jnp.abs(value))
    series = tail * (1.0 - tail * (0.5 - tail * (1.0 / 3.0 - 0.25 * tail)))
    return jnp.maximum(value, 0.0) + jnp.where(tail < 0.01, series, jnp.log(1.0 + tail))


def iota(shape, dim):
    return lax.broadcasted_iota(jnp.int32, shape, dim)


def span_scalars(info, m):
    first = info[2 * m]
    start = ((first + (BLOCK - 1)) >> 7) << 7
    return first, start, start + info[2 * m + 1], info[2 * MB], info[2 * MB + 1]


def keeps(info, m):
    _, start, _, base, span = span_scalars(info, m)

    def keep(position):
        begins = (position == 0) | (position == start) | (position >= span)
        return jnp.where(begins, 0.0, 1.0).astype(F32)

    forward = [keep(base), keep(base + BLOCK)]
    reverse = [keep(base + BLOCK), keep(base + 2 * BLOCK)]
    return forward, reverse


def row_masks(info, m, shape, offset=0):
    first, start, end, base, _ = span_scalars(info, m)
    place = iota(shape, 0) + (base + offset)
    inside = (place < first) | ((place >= start) & (place < end))
    offset = jnp.where(place >= start, place - start, place)
    return inside.astype(F32), [(offset >= k).astype(F32) for k in range(CONV)]


def conv_windows(ref, cols):
    main = ref[0, :TOK_DEV, cols]
    halo = ref[0, TOK_DEV:, cols]
    whole = jnp.concatenate([halo, main], axis=0)
    return [main] + [whole[HALO - k : HALO - k + TOK_DEV] for k in range(1, CONV)]


def conv_value(windows, masks, taps, cols):
    value = taps[CONV : CONV + 1, cols] + taps[0:1, cols] * windows[0]
    for k in range(1, CONV):
        value = value + taps[k : k + 1, cols] * (windows[k] * masks[k])
    return value


def gather_kernel(
    count, columns, info, x_in, cot_in, w_inner, w_state, w_step, mine,
    w_all, hidden, hidden_t, d_branch, d_branch_t, norm, taps, steps, skip, scale, spread_f, spread_r, sum_f, sum_r,
    halo, small, skip_row, halo_sems, small_sems, x_sems, y_sems, mate_sems, own_sems,
):
    me, part = lax.axis_index("dp"), lax.axis_index("fsdp")
    side, core, column = lax.rem(me, 2), lax.rem(part, 2), part // 2
    partner, mate = me + 1 - 2 * side, part + 1 - 2 * core
    has_next, has_last = me < count - 1, me > 0
    shards = 2 * columns
    rows = w_inner.shape[0]
    chunk = rows // (2 * CUTS)

    barrier = pltpu.get_barrier_semaphore()

    @pl.when(has_next)
    def _():
        pl.semaphore_signal(barrier, inc=1, device_id={"dp": me + 1})

    @pl.when(has_last)
    def _():
        pl.semaphore_signal(barrier, inc=1, device_id={"dp": me - 1})

    def other(d):
        return lax.rem(part + d + shards, shards)

    def column_at(d):
        return lax.rem(column + d + columns, columns)

    for d in range(1, shards):
        pl.semaphore_signal(barrier, inc=1, device_id={"fsdp": other(d)})
    pl.semaphore_wait(barrier, shards - 1 + has_next.astype(jnp.int32) + has_last.astype(jnp.int32))

    def remote(source, target, sems, k, where):
        return pltpu.make_async_remote_copy(
            src_ref=source, dst_ref=target, send_sem=sems.at[0, k], recv_sem=sems.at[1, k], device_id=where
        )

    def rows_of(owner, half, k):
        return w_all.at[pl.ds(pl.multiple_of(owner * rows + half * (rows // 2) + k * chunk, 16), chunk)]

    edge = remote(x_in.at[:, pl.ds(TOK_DEV - 2 * HALO, 2 * HALO)], halo, halo_sems, 0, {"dp": me + 1})

    def small_copy(d, theirs):
        return remote(mine, small.at[other(-d) if theirs else part], small_sems, d, {"fsdp": other(d)})

    def x_copy(k, d):
        at = rows_of(part, side, k)
        return remote(at, at, x_sems, k * columns + d, {"fsdp": 2 * column_at(d) + core})

    def x_arrival(k, d):
        at = rows_of(2 * column_at(-d) + core, side, k)
        return remote(at, at, x_sems, k * columns + d, {"fsdp": part})

    def y_copy(k, d, theirs):
        at = rows_of(2 * column_at(-d) + core, 1 - side if theirs else side, k)
        return remote(at, at, y_sems, k * columns + d, {"dp": partner})

    def mate_copy(k, d, half, theirs):
        at = rows_of(2 * column_at(-d) + (1 - core if theirs else core), half, k)
        return remote(at, at, mate_sems, (k * columns + d) * 2 + half, {"fsdp": mate})

    def own_copy(owner):
        at = w_all.at[pl.ds(pl.multiple_of(owner * rows, 16), rows)]
        return remote(at, at, own_sems, 0, {"fsdp": mate})

    @pl.when(has_next)
    def _():
        edge.start()

    for d in range(1, shards):
        small_copy(d, False).start()
    here = pl.ds(pl.multiple_of(part * rows, 16), rows)
    w_all[here, : 2 * INNER] = w_inner[...]
    w_all[here, 2 * INNER : 2 * INNER + 2 * STATE] = w_state[...]
    w_all[here, 2 * INNER + 2 * STATE :] = jnp.concatenate(
        [w_step[...].astype(F32), jnp.zeros((rows, LANES - 2 * HEADS), F32)], axis=1
    ).astype(BF16)
    for k in range(2):
        for d in range(1, columns):
            x_copy(k, d).start()
    own_copy(part).start()

    @pl.when(me == 0)
    def _():
        halo[...] = jnp.zeros_like(halo)

    def chosen(mask):
        return jnp.where(mask, 1.0, 0.0).astype(BF16)

    shape = (2 * LANES, INNER)
    lane_of, head_of = iota(shape, 0) & (LANES - 1), iota(shape, 1) >> 6
    spread_f[...] = chosen(lane_of == head_of)
    spread_r[...] = chosen(lane_of == head_of + HEADS)
    shape = (INNER, LANES)
    lane_of, head_of = iota(shape, 1), iota(shape, 0) >> 6
    sum_f[...] = chosen(lane_of == head_of)
    sum_r[...] = chosen(lane_of == head_of + HEADS)
    for m in range(MB):
        valid = row_masks(info, m, (TOK_DEV, D))[0]
        value = jnp.where(valid > 0.0, cot_in[m].astype(F32), 0.0)
        d_branch[m] = value.astype(BF16)
        d_branch_t[:, m * TOK_DEV : (m + 1) * TOK_DEV] = jnp.transpose(value).astype(BF16)

    for ref in (norm, taps, steps, skip_row):
        ref[...] = jnp.zeros_like(ref)
    for d in range(1, shards):
        small_copy(d, True).wait_recv()
    small[part] = mine[...]
    wide, heads = CONV_COLS // shards, HEADS // shards
    for f in range(shards):
        value = small[f].astype(F32)
        taps[: CONV + 1, f * wide : (f + 1) * wide] = value[: CONV + 1, :wide]
        gain = value[5:6, : INNER // shards]
        scale[:, f * INNER // shards : (f + 1) * INNER // shards] = jnp.broadcast_to(gain, (8, INNER // shards))
        norm[:, f * rows : (f + 1) * rows] = value[6:7, :rows]
        steps[0:1, 2 * f * heads : 2 * (f + 1) * heads] = value[7:8, : 2 * heads]
        rates = jnp.exp(value[8:9, :heads])
        steps[1:2, f * heads : (f + 1) * heads] = rates
        steps[1:2, HEADS + f * heads : HEADS + (f + 1) * heads] = rates
        skip_row[0:1, f * heads : (f + 1) * heads] = value[9:10, :heads]
    skip[...] = dot(spread_operand(skip_row[...]), spread_f[...])

    @pl.when(has_last)
    def _():
        edge.wait_recv()

    def normalise(values):
        root = lax.rsqrt(jnp.mean(values * values, axis=1, keepdims=True) + EPSILON)
        return values * root * norm[...]

    def hide(m):
        value = normalise(x_in[m].astype(F32))
        hidden[m, :TOK_DEV] = value.astype(BF16)
        hidden_t[:, m * TOK_DEV : (m + 1) * TOK_DEV] = jnp.transpose(value).astype(BF16)
        hidden[m, TOK_DEV:] = normalise(halo[m].astype(F32)[HALO:]).astype(BF16)

    def pass_on(k):
        for d in range(1, columns):
            y_copy(k, d, True).wait_recv()

            @pl.when(side == 0)
            def _():
                mate_copy(k, d, 1, False).start()

            @pl.when(side == 1)
            def _():
                mate_copy(k, d, 0, False).start()

    for k in range(CUTS):
        if k < MB:
            hide(k)
        for d in range(1, columns):
            x_arrival(k, d).wait_recv()
            y_copy(k, d, False).start()

            @pl.when(side == 0)
            def _():
                mate_copy(k, d, 0, False).start()

            @pl.when(side == 1)
            def _():
                mate_copy(k, d, 1, False).start()

            if k + 2 < CUTS:
                x_copy(k + 2, d).start()
        if k > 0:
            pass_on(k - 1)
    for m in range(CUTS, MB):
        hide(m)
    pass_on(CUTS - 1)
    own_copy(mate).wait_recv()
    own_copy(part).wait_send()
    for k in range(CUTS):
        for d in range(1, columns):
            for half in range(2):
                mate_copy(k, d, half, True).wait_recv()
                mate_copy(k, d, half, False).wait_send()
            x_copy(k, d).wait_send()
            y_copy(k, d, False).wait_send()
    for d in range(1, shards):
        small_copy(d, False).wait_send()

    @pl.when(has_next)
    def _():
        edge.wait_send()


def gather_weights(info, x, cot, w_inner, w_state, w_step, mine, identity):
    count, shards = lax.axis_size("dp"), lax.axis_size("fsdp")
    columns = shards // 2
    whole = pl.BlockSpec(memory_space=pltpu.VMEM)
    pairs = CUTS * columns
    return pl.pallas_call(
        partial(gather_kernel, count, columns),
        in_specs=[SCALARS] + [whole] * 6,
        out_specs=[whole] * 14,
        out_shape=[
            struct(D, WIDE, dtype=BF16), struct(MB, TOK_DEV + HALO, D, dtype=BF16), struct(D, MB * TOK_DEV, dtype=BF16),
            struct(MB, TOK_DEV, D, dtype=BF16), struct(D, MB * TOK_DEV, dtype=BF16), struct(1, D), struct(8, CONV_COLS), struct(8, LANES), struct(8, INNER), struct(8, INNER),
            struct(2 * LANES, INNER, dtype=BF16), struct(2 * LANES, INNER, dtype=BF16),
            struct(INNER, LANES, dtype=BF16), struct(INNER, LANES, dtype=BF16),
        ],
        scratch_shapes=[
            pltpu.VMEM((MB, 2 * HALO, D), BF16), pltpu.VMEM((shards,) + mine.shape, BF16), pltpu.VMEM((8, LANES), F32),
            pltpu.SemaphoreType.DMA((2, 1)), pltpu.SemaphoreType.DMA((2, shards)), pltpu.SemaphoreType.DMA((2, pairs)),
            pltpu.SemaphoreType.DMA((2, pairs)), pltpu.SemaphoreType.DMA((2, 2 * pairs)), pltpu.SemaphoreType.DMA((2, 1)),
        ],
        compiler_params=pltpu.CompilerParams(vmem_limit_bytes=VMEM_LIMIT, collective_id=identity, has_side_effects=True),
    )(info, x, cot, w_inner, w_state, w_step, mine)


def front_body(m, info, vals, bc, dt, taps, steps, spread_f, spread_r, v_out, bc_out, fr_out, frp_out, tot_f, tot_r, kept_f, kept_r, dx_out):
    valid, masks = row_masks(info, m, (TOK_DEV, LANES))
    for chunk in range(PAIRS + 1):
        cols = pl.ds(chunk * LANES, LANES)
        source, own = (vals, cols) if chunk < PAIRS else (bc, pl.ds(0, LANES))
        value = conv_value(conv_windows(source, own), masks, taps, cols)
        value = valid * (value * sigmoid(value))
        if chunk < PAIRS:
            v_out[m, :, cols] = value.astype(BF16)
        else:
            bc_out[m] = value
    lane = iota((BLOCK, LANES), 1)
    rows = iota((BLOCK, BLOCK), 0)
    columns = iota((BLOCK, BLOCK), 1)
    lower = (rows >= columns).astype(F32)
    upper = (rows <= columns).astype(F32)
    forward, reverse = keeps(info, m)
    ends = []
    tails = []
    inputs = []
    for b in range(2):
        span = pl.ds(b * BLOCK, BLOCK)
        step = softplus(dt[0, span, :] + steps[0:1, :])
        log = -step * steps[1:2, :]
        summed = jnp.where(lane < HEADS, dot(lower, log, precision=HIGHEST), dot(upper, log, precision=HIGHEST))
        shifted = summed - jnp.log(step)
        fr_out[m, span, :] = summed
        frp_out[m, span, :] = shifted
        end = jnp.where(lane[:1] < HEADS, summed[BLOCK - 1 :], summed[:1])
        ends.append(jnp.exp(end))
        tails.append(spread_operand(jnp.where(lane < 2 * HEADS, jnp.exp(end - shifted), 0.0)))
        acts = bc_out[m, span, :]
        inputs.append(twice(jnp.transpose(by_lane(acts, swapped(acts))).astype(BF16), 1))
    ends = spread_operand(jnp.concatenate(ends + [jnp.zeros((6, LANES), F32)], axis=0))
    width = 2 * LANES
    for chunk in range(INNER // width):
        cols = pl.ds(chunk * width, width)
        decay_f = dot(ends, spread_f[:, cols])
        decay_r = dot(ends, spread_r[:, cols])
        parts_f = []
        parts_r = []
        for b in range(2):
            v = v_out[m, pl.ds(b * BLOCK, BLOCK), cols].astype(F32)
            parts_f.append(fold(dot(inputs[b], stacked(dot(tails[b], spread_f[:, cols]) * v))))
            parts_r.append(fold(dot(inputs[b], stacked(dot(tails[b], spread_r[:, cols]) * v))))
        kept_f[m, :, cols] = parts_f[0]
        kept_r[m, :, cols] = parts_r[1]
        total_f = parts_f[1] + (forward[1] * decay_f[1:2]) * parts_f[0]
        total_r = parts_r[0] + (reverse[0] * decay_r[0:1]) * parts_r[1]
        for k in range(PARTS):
            part = slice(k * STATE // PARTS, (k + 1) * STATE // PARTS)
            tot_f[PARTS * m + k, :, cols] = total_f[part]
            tot_r[PARTS * m + k, :, cols] = total_r[part]
        dx_out[m, 0:2, cols] = decay_f[0:2]
        dx_out[m, 2:4, cols] = decay_r[0:2]
        dx_out[m, 4:5, cols] = (forward[0] * forward[1]) * (decay_f[0:1] * decay_f[1:2])
        dx_out[m, 5:6, cols] = (reverse[0] * reverse[1]) * (decay_r[0:1] * decay_r[1:2])
        dx_out[m, 6:8, cols] = jnp.zeros((2, width), F32)


def stacked(value):
    return jnp.concatenate(halves(value), axis=0)


def doubled(value):
    high, low = halves(value)
    return jnp.concatenate([high, high, low, low], axis=0)


def pair_stack(value):
    lane = iota(value.shape, 1)
    zero = jnp.zeros_like(value)
    return jnp.concatenate([jnp.where(lane < HEAD_DIM, value, zero), jnp.where(lane < HEAD_DIM, zero, value)], axis=0)


def swapped(value):
    return pltpu.roll(value, STATE, axis=1)


def intra_body(m, b, v, bc, fr, frp, skip, y_out):
    span = pl.ds(pl.multiple_of(b * BLOCK, BLOCK), BLOCK)
    rows = iota((BLOCK, BLOCK), 0)
    columns = iota((BLOCK, BLOCK), 1)
    lower = rows > columns
    acts = bc[m, span, :]
    outs = jnp.where(columns < STATE, swapped(acts), 0.0)
    scores = jnp.where(rows == columns, 0.0, dot(outs, acts, COLS, HIGHEST))
    cum = fr[m, span, :]
    shifted = jnp.transpose(frp[m, span, :])
    for pair in range(PAIRS):
        mats = []
        for h in (2 * pair, 2 * pair + 1):
            r = HEADS + h
            gap = jnp.where(lower, cum[:, h : h + 1] - shifted[h : h + 1], cum[:, r : r + 1] - shifted[r : r + 1])
            mats.append((jnp.exp(gap) * scores).astype(BF16))
        cols = pl.ds(pair * LANES, LANES)
        value = v[m, span, cols]
        y = dot(jnp.concatenate(mats, axis=1), pair_stack(value))
        y_out[0, :, cols] = y + skip[0:1, cols] * value.astype(F32)


def entering(m, b, cols, forward, reverse, enter_f, enter_r, kept_f, kept_r, dx):
    first_f = forward[0] * jnp.concatenate([enter_f[PARTS * m + k, :, cols] for k in range(PARTS)], axis=0)
    last_r = reverse[1] * jnp.concatenate([enter_r[PARTS * m + k, :, cols] for k in range(PARTS)], axis=0)
    state_f = jnp.where(b == 0, first_f, forward[1] * (dx[m, 0:1, cols] * first_f + kept_f[m, :, cols]))
    state_r = jnp.where(b == 1, last_r, reverse[0] * (dx[m, 3:4, cols] * last_r + kept_r[m, :, cols]))
    return state_f, state_r


def middle_body(
    slot, info, y, gate, d_normed, v, bc, fr, enter_f, enter_r, kept_f, kept_r, dx, gain, spread_f, spread_r, sum_f, sum_r,
    normed, d_mixed, d_gate, back_f, back_r, leave_f, leave_r, d_outs, read_out, d_gain, d_skip, mixed_s, part_f, part_r, exp_f, exp_r,
):
    m, b = slot // 2, lax.rem(slot, 2)
    span = pl.ds(pl.multiple_of(b * BLOCK, BLOCK), BLOCK)
    forward, reverse = keeps(info, m)
    lane = iota((BLOCK, LANES), 1)
    acts = bc[m, span, :]
    outs = by_lane(swapped(acts), acts)
    outs_t = twice(jnp.transpose(outs).astype(BF16), 1)
    outs = twice(outs.astype(BF16), 1)
    grown = spread_operand(jnp.where(lane < 2 * HEADS, jnp.exp(fr[m, span, :]), 0.0))
    width = 2 * LANES
    chunks = INNER // width
    squares = jnp.zeros((BLOCK, 1), F32)
    cross = jnp.zeros((BLOCK, 1), F32)
    for chunk in range(chunks):
        cols = pl.ds(chunk * width, width)
        state_f, state_r = entering(m, b, cols, forward, reverse, enter_f, enter_r, kept_f, kept_r, dx)
        ef = dot(grown, spread_f[:, cols])
        er = dot(grown, spread_r[:, cols])
        carried_f = ef * dot(outs, doubled(state_f))
        carried_r = er * dot(outs, doubled(state_r))
        mixed = y[0, :, cols] + carried_f + carried_r
        exp_f[:, cols] = ef
        exp_r[:, cols] = er
        part_f[:, cols] = carried_f
        part_r[:, cols] = carried_r
        mixed_s[:, cols] = mixed
        g = gate[0, :, cols]
        gated = mixed * (g * sigmoid(g))
        squares = squares + jnp.sum(gated * gated, axis=1, keepdims=True)
        cross = cross + jnp.sum(gated * gain[0:1, cols] * d_normed[0, :, cols], axis=1, keepdims=True)
    scale = lax.rsqrt(squares * (1.0 / INNER) + EPSILON)
    pull = scale * scale * scale * (cross * (1.0 / INNER))
    d_o = jnp.zeros((BLOCK, LANES), F32)
    reads = jnp.zeros((BLOCK, LANES), F32)

    @pl.when((m == 0) & (b == 0))
    def _():
        d_gain[...] = jnp.zeros_like(d_gain)
        d_skip[...] = jnp.zeros_like(d_skip)

    @pl.when(b == 0)
    def _():
        for k in range(PARTS):
            leave_f[PARTS * m + k] = jnp.zeros(CARRY_SHAPE[1:], F32)
            leave_r[PARTS * m + k] = jnp.zeros(CARRY_SHAPE[1:], F32)

    for chunk in range(chunks):
        cols = pl.ds(chunk * width, width)
        g = gate[0, :, cols]
        sig = sigmoid(g)
        silu = g * sig
        mixed = mixed_s[:, cols]
        gated = mixed * silu
        dy = d_normed[0, :, cols]
        scaled = gated * scale
        normed[m, span, cols] = (scaled * gain[0:1, cols]).astype(BF16)
        d_gain[0:1, cols] += jnp.sum(dy * scaled, axis=0, keepdims=True)
        d_gated = scale * gain[0:1, cols] * dy - gated * pull
        dm = d_gated * silu
        d_gate[m, span, cols] = (d_gated * mixed * sig * (1.0 + g * (1.0 - sig))).astype(BF16)
        d_mixed[slot, :, cols] = dm.astype(BF16)
        d_skip[0:1, cols] += jnp.sum(dm * v[m, span, cols].astype(F32), axis=0, keepdims=True)
        state_f, state_r = entering(m, b, cols, forward, reverse, enter_f, enter_r, kept_f, kept_r, dx)
        grown_f = exp_f[:, cols] * dm
        grown_r = exp_r[:, cols] * dm
        local_f = fold(dot(outs_t, stacked(grown_f)))
        local_r = fold(dot(outs_t, stacked(grown_r)))
        back_f[0, 0, :, cols] = local_f
        back_r[0, 0, :, cols] = local_r
        weight_f = jnp.where(b == 0, forward[0], (forward[0] * forward[1]) * dx[m, 0:1, cols])
        weight_r = jnp.where(b == 0, (reverse[0] * reverse[1]) * dx[m, 3:4, cols], reverse[1])
        local_f = weight_f * local_f
        local_r = weight_r * local_r
        for k in range(PARTS):
            part = slice(k * STATE // PARTS, (k + 1) * STATE // PARTS)
            leave_f[PARTS * m + k, :, cols] += local_f[part]
            leave_r[PARTS * m + k, :, cols] += local_r[part]
        d_o = d_o + dot(spread_operand(grown_f), twice(stacked(state_f), 1), COLS)
        d_o = d_o + dot(spread_operand(grown_r), twice(stacked(state_r), 1), COLS)
        reads = reads + head_sums(dm * part_f[:, cols], sum_f[cols, :]) + head_sums(dm * part_r[:, cols], sum_r[cols, :])
    d_outs[slot] = jnp.where(lane < STATE, 0.0, d_o + swapped(d_o))
    read_out[slot] = reads


def intra_back_body(slot, v, d_mixed, bc, fr, frp, skip, d_outs, read_out, d_v, d_bc, sums, d_log, row_s, turn):
    m, b = slot // 2, lax.rem(slot, 2)
    span = pl.ds(pl.multiple_of(b * BLOCK, BLOCK), BLOCK)
    rows = iota((BLOCK, BLOCK), 0)
    columns = iota((BLOCK, BLOCK), 1)
    ahead = rows < columns
    acts = bc[m, span, :]
    low = columns < STATE
    turned = swapped(acts)
    outs = jnp.where(low, turned, 0.0)
    scores = jnp.where(rows == columns, 0.0, dot(acts, outs, COLS, HIGHEST))
    cum = jnp.transpose(fr[m, span, :])
    shifted = frp[m, span, :]
    d_scores = jnp.zeros((BLOCK, BLOCK), F32)
    gathered = jnp.zeros((BLOCK, LANES), F32)

    row_s[...] = jnp.zeros_like(row_s)
    for pair in range(PAIRS):
        cols = pl.ds(pair * LANES, LANES)
        value = v[m, span, cols]
        dm = d_mixed[slot, :, cols]
        products = dot(pair_stack(value), dm, COLS)
        mats = []
        for side in range(2):
            h = 2 * pair + side
            r = HEADS + h
            gap = jnp.where(ahead, cum[h : h + 1] - shifted[:, h : h + 1], cum[r : r + 1] - shifted[:, r : r + 1])
            weight = jnp.exp(gap)
            mats.append((weight * scores).astype(BF16))
            reach = products[side * BLOCK : (side + 1) * BLOCK] * weight
            d_scores = d_scores + reach
            both = reach * scores
            first = jnp.where(ahead, both, 0.0)
            second = both - first
            gathered = jnp.where(columns == h, jnp.sum(first, axis=1, keepdims=True), gathered)
            gathered = jnp.where(columns == r, jnp.sum(second, axis=1, keepdims=True), gathered)
            row_s[h : h + 1, :] = jnp.sum(first, axis=0, keepdims=True)
            row_s[r : r + 1, :] = jnp.sum(second, axis=0, keepdims=True)
        dmf = dm.astype(F32)
        d_v[0, :, cols] = dot(jnp.concatenate(mats, axis=1), pair_stack(dm)) + skip[0:1, cols] * dmf
        if pair % TURN_PAIRS == TURN_PAIRS - 1:
            turn(pair // TURN_PAIRS)
    d_scores = jnp.where(rows == columns, 0.0, d_scores)
    ins = jnp.where(low, 0.0, turned)
    d_bc[0] = dot(d_scores, outs, precision=HIGHEST) + dot(jnp.transpose(d_scores), ins, precision=HIGHEST) + d_outs[slot]
    sums[0] = gathered
    d_log[0] = jnp.transpose(row_s[...]) - gathered + read_out[slot]


def shard_steps(columns, normed, d_branch_t, hidden_t, d_gate, outs, buffers):
    put, gots, cross_puts, cross_gots, mate_sems, cross_sems = buffers
    part = lax.axis_index("fsdp")
    core, column = lax.rem(part, 2), part // 2
    mate = part + 1 - 2 * core
    rows = put.shape[1]

    def column_at(d):
        return lax.rem(column + d + columns, columns)

    def remote(source, target, sems, k, device):
        return pltpu.make_async_remote_copy(
            src_ref=source, dst_ref=target, send_sem=sems.at[0, k], recv_sem=sems.at[1, k], device_id={"fsdp": device}
        )

    def to_mate(which, x):
        return remote(put.at[x], gots[which].at[x], mate_sems, which * columns + x, mate)

    def across(which, d):
        target = 2 * column_at(d) + core
        return remote(cross_puts[which].at[d - 1], cross_gots[which].at[d - 1], cross_sems, which * columns + d, target)

    def piece(which, owner, h):
        half = rows // 2
        if which == 0:
            group = 1 if rows % LANES == 0 else 2
            at = pl.ds(pl.multiple_of((owner // group) * (group * rows), LANES), group * rows)
            total = sum(
                dot(d_branch_t[h * rows : (h + 1) * rows, m * TOK_DEV : (m + 1) * TOK_DEV], normed[m, :, at]) for m in range(MB)
            )
            return total if group == 1 else jnp.where(lax.rem(owner, 2) == 0, total[:, :rows], total[:, rows:])
        at = pl.ds(pl.multiple_of(owner * half, 16), half)
        return sum(
            dot(hidden_t[at, m * TOK_DEV : (m + 1) * TOK_DEV], d_gate[m, :, h * D : (h + 1) * D]) for m in range(MB)
        )

    def view(which, h):
        return (slice(None), slice(h * rows, (h + 1) * rows)) if which == 0 else (slice(h * rows // 2, (h + 1) * rows // 2),)

    def count(which):
        return D // rows if which == 0 else 2

    def greet(barrier):
        pl.semaphore_signal(barrier, inc=1, device_id={"fsdp": mate})
        for d in range(1, columns):
            pl.semaphore_signal(barrier, inc=1, device_id={"fsdp": 2 * column_at(d) + core})
        return columns

    def foreign(which):
        for x in range(columns):
            if which == 1:
                to_mate(0, x).wait_send()
            for h in range(count(which)):
                put[(x,) + view(which, h)] = piece(which, 2 * x + 1 - core, h).astype(BF16)
            to_mate(which, x).start()

    def local(which):
        for x in range(columns):
            to_mate(which, x).wait_recv()
        for d in list(range(1, columns)) + [0]:
            x = column_at(d)
            for h in range(count(which)):
                at = view(which, h)
                value = piece(which, 2 * x + core, h) + gots[which][(x,) + at].astype(F32)
                if d == 0:
                    outs[which][at] = value
                else:
                    cross_puts[which][(d - 1,) + at] = value.astype(BF16)
            if d > 0:
                across(which, d).start()

    def close():
        for which in range(2):
            for d in range(1, columns):
                across(which, d).wait()
                outs[which][...] += cross_gots[which][d - 1].astype(F32)
        for x in range(columns):
            to_mate(1, x).wait_send()

    return greet, foreign, local, close


def shard_buffers(shards):
    columns, shape = shards // 2, (INNER // shards, D)
    low, few = pltpu.VMEM((columns,) + shape, BF16), pltpu.VMEM((columns - 1,) + shape, BF16)
    return [low] * 3 + [few] * 4 + [pltpu.SemaphoreType.DMA((2, 2 * columns))] * 2


def gather_steps(columns, w_out, w_back, w_back_out, cross_sems, mate_sems, out_sems):
    part = lax.axis_index("fsdp")
    core, column = lax.rem(part, 2), part // 2
    mate = part + 1 - 2 * core
    rows = w_out.shape[0]

    def column_at(d):
        return lax.rem(column + d + columns, columns)

    def copy(sems, k, owner, device):
        at = w_back.at[pl.ds(pl.multiple_of(owner * rows, LANES // 2), rows)]
        return pltpu.make_async_remote_copy(
            src_ref=at, dst_ref=at, send_sem=sems.at[0, k], recv_sem=sems.at[1, k], device_id={"fsdp": device}
        )

    def across(d, theirs):
        return copy(cross_sems, d, 2 * column_at(-d) + core if theirs else part, 2 * column_at(d) + core)

    def to_mate(d, theirs):
        return copy(mate_sems, d, 2 * column_at(-d) + (1 - core if theirs else core), mate)

    def keep():
        return pltpu.make_async_copy(w_back, w_back_out, out_sems.at[0])

    def start():
        here = w_back.at[pl.ds(pl.multiple_of(part * rows, LANES // 2), rows)]
        own = pltpu.make_async_copy(w_out, here, out_sems.at[1])
        own.start()
        own.wait()
        for d in range(1, columns):
            across(d, False).start()
        to_mate(0, False).start()

    def forward():
        for d in range(1, columns):
            across(d, True).wait_recv()
            to_mate(d, False).start()

    def arrive():
        for d in range(columns):
            to_mate(d, True).wait_recv()
        keep().start()

    def close():
        keep().wait()
        for d in range(columns):
            to_mate(d, False).wait_send()
            if d > 0:
                across(d, False).wait_send()

    return start, forward, arrive, close


def mixer_kernel(
    levels, columns, info, vals, bc_in, dt, gate, taps, rates, spread_f, spread_r, sum_f, sum_r, skip, gain, w_out, d_branch_in, d_branch_t_in, hidden_t_in,
    v_out, bc_out, fr_out, frp_out, kept_f_out, kept_r_out, dx_out, normed_out, d_gate_out,
    back_f, back_r, d_gain, d_skip, d_v, d_bc, sums, d_log, first_out, second_out, enter_f, enter_r, after_f, after_r, w_back_out,
    v, bc, fr, frp, kept_f, kept_r, dx, normed, d_gate, d_branch, d_branch_t, hidden_t, load_sems, front_sems, middle_sems, y, d_normed, mixed_s, part_f, part_r, exp_f, exp_r, row_s, d_mixed, d_outs, read_out, w_back, w_cross, w_mate, w_kept,
    put, got_1, got_2, cross_put_1, cross_put_2, cross_got_1, cross_got_2, mate_sems, cross_sems,
    gains_other, gain_sems, tot_f, tot_r, leave_f, leave_r, *buffers,
):
    s = pl.program_id(0)
    half = len(buffers) // 2
    greet_dp, begin, send_gains, gains_here, send, run, end, total = carry_steps(
        levels, 4, 5, dx, gains_other, gain_sems, tot_f, tot_r, enter_f, enter_r, buffers[:half]
    )
    _, begin_back, _, _, send_back, run_back, end_back, _ = carry_steps(
        levels, 5, 4, dx, gains_other, gain_sems, leave_r, leave_f, after_r, after_f, buffers[half:]
    )
    greet, foreign, local, close = shard_steps(
        columns, normed, d_branch_t, hidden_t, d_gate, (first_out, second_out),
        (put, (got_1, got_2), (cross_put_1, cross_put_2), (cross_got_1, cross_got_2), mate_sems, cross_sems),
    )
    w_start, w_forward, w_arrive, w_close = gather_steps(columns, w_out, w_back, w_back_out, w_cross, w_mate, w_kept)
    entered_f, entered_r = buffers[0], buffers[1]
    fronts = ((v, v_out), (bc, bc_out), (fr, fr_out), (frp, frp_out), (kept_f, kept_f_out), (kept_r, kept_r_out), (dx, dx_out))

    def front_copy(i, m):
        return pltpu.make_async_copy(fronts[i][0].at[m], fronts[i][1].at[m], front_sems.at[i, m])

    def middle_copy(i, slot):
        ref, out = ((normed, normed_out), (d_gate, d_gate_out))[i]
        m, span = slot // 2, pl.ds(pl.multiple_of(lax.rem(slot, 2) * BLOCK, BLOCK), BLOCK)
        return pltpu.make_async_copy(ref.at[m, span], out.at[m, span], middle_sems.at[i, slot])

    def load(i):
        return pltpu.make_async_copy(*((d_branch_in, d_branch), (hidden_t_in, hidden_t), (d_branch_t_in, d_branch_t))[i], load_sems.at[i])

    middle, back = MB, 3 * MB
    window = 5

    @pl.when(s == 0)
    def _():
        barrier = pltpu.get_barrier_semaphore()
        pl.semaphore_wait(barrier, greet(barrier) + greet_dp(barrier))
        for i in range(3):
            load(i).start()
        begin()
        begin_back()
        w_start()

    @pl.when(s < middle)
    def _():
        front_body(s, info, vals, bc_in, dt, taps, rates, spread_f, spread_r, v, bc, fr, frp, tot_f, tot_r, kept_f, kept_r, dx)
        send_gains(s)
        for i in range(len(fronts)):
            front_copy(i, s).start()

        for m, (low, high) in enumerate(((0, 2), (2, 4), (4, window))):

            @pl.when(s == m)
            def _():
                send(low, high)

    done = 0
    for slot in range(2 * MB):
        need = min(PARTS + LAG * (levels - 1) + slot * (PARTS // 2), total)

        @pl.when(s == middle + slot)
        def _():
            if slot == 0:
                for m in range(MB):
                    gains_here(m)
                w_forward()
            run(done, need, window)
            if slot == 0:
                for i in range(3):
                    load(i).wait()
                w_arrive()

        done = need

    @pl.when((s >= middle) & (s < back))
    def _():
        slot = s - middle
        m, b = slot // 2, lax.rem(slot, 2)
        intra_body(m, b, v, bc, fr, frp, skip, y)
        d_normed[0] = dot(d_branch[m, pl.ds(pl.multiple_of(b * BLOCK, BLOCK), BLOCK), :], w_back[...], COLS)
        middle_body(
            slot, info, y, gate, d_normed, v, bc, fr, entered_f, entered_r, kept_f, kept_r, dx, gain, spread_f, spread_r, sum_f, sum_r,
            normed, d_mixed, d_gate, back_f, back_r, leave_f, leave_r, d_outs, read_out, d_gain, d_skip, mixed_s, part_f, part_r, exp_f, exp_r,
        )

        middle_copy(0, slot).start()
        middle_copy(1, slot).start()

        @pl.when(b == 1)
        def _():
            send_back(PARTS * m, PARTS * (m + 1))

    for k, step in enumerate((foreign, local)):
        for which in range(2):

            @pl.when(s == back + 2 * which + k)
            def _():
                step(which)

    @pl.when(s >= back)
    def _():
        slot = s - back
        each = -(-total // (2 * MB * TURNS))

        def turn(k):
            at = slot * TURNS + k
            run_back(at * each, (at + 1) * each, 0)

        intra_back_body(slot, v, d_mixed, bc, fr, frp, skip, d_outs, read_out, d_v, d_bc, sums, d_log, row_s, turn)

    @pl.when(s == 5 * MB - 1)
    def _():
        close()
        w_close()
        for m in range(MB):
            for i in range(len(fronts)):
                front_copy(i, m).wait()

        @pl.loop(0, 2 * MB)
        def _(slot):
            middle_copy(0, slot).wait()
            middle_copy(1, slot).wait()

        end(True)
        end_back(False)


def final_kernel(
    levels, info, vals, bc_in, dt, taps, rates, v, bc, fr, frp, enter_f, enter_r, kept_f, kept_r, dx, after_f, after_r, back_f, back_r,
    d_v, d_bc, sums, d_log, spread_f, spread_r, sum_f, sum_r, first_in, second_in,
    late, before, last, d_taps, d_small, first_out, second_out, d_acts, *buffers,
):
    m = pl.program_id(0)
    forward, reverse = keeps(info, m)
    if levels:
        greet, steps = sum_steps(levels, (buffers[:6], buffers[6:12]), *buffers[12:])

    def beside(at, *todo):
        if levels:

            @pl.when(m == at)
            def _():
                for stage, i in todo:
                    steps[stage](i)

    if levels:

        @pl.when(m == 0)
        def _():
            barrier = pltpu.get_barrier_semaphore()
            pl.semaphore_wait(barrier, greet(barrier))
            buffers[0][...] = first_in[...]
            buffers[6][...] = second_in[...]

    beside(0, (0, 0))
    lane = iota((BLOCK, LANES), 1)
    row = iota((BLOCK, LANES), 0)
    rows = iota((BLOCK, BLOCK), 0)
    columns = iota((BLOCK, BLOCK), 1)
    lower = (rows >= columns).astype(F32)
    upper = (rows <= columns).astype(F32)
    width = 2 * LANES

    @pl.when(m == 0)
    def _():
        d_taps[...] = jnp.zeros_like(d_taps)
        d_small[...] = jnp.zeros_like(d_small)

    for b in range(2):
        span = pl.ds(b * BLOCK, BLOCK)
        summed = fr[0, span, :]
        end = jnp.where(lane[:1] < HEADS, summed[BLOCK - 1 :], summed[:1])
        tail = spread_operand(jnp.where(lane < 2 * HEADS, jnp.exp(end - frp[0, span, :]), 0.0))
        acts = bc[0, span, :]
        ins = twice(by_lane(acts, swapped(acts)).astype(BF16), 1)
        d_in = jnp.zeros((BLOCK, LANES), F32)
        used = jnp.zeros((BLOCK, LANES), F32)
        decays = jnp.zeros((8, LANES), F32)
        for chunk in range(INNER // width):
            cols = pl.ds(chunk * width, width)
            grad_f = jnp.concatenate([after_f[k, :, cols] for k in range(PARTS)], axis=0)
            grad_r = jnp.concatenate([after_r[k, :, cols] for k in range(PARTS)], axis=0)
            if b == 0:
                grad_f = forward[1] * (back_f[0, 1, :, cols] + dx[0, 1:2, cols] * grad_f)
            else:
                grad_r = reverse[0] * (back_r[0, 0, :, cols] + dx[0, 2:3, cols] * grad_r)
            state_f, state_r = entering(0, b, cols, forward, reverse, enter_f, enter_r, kept_f, kept_r, dx)
            tail_f = dot(tail, spread_f[:, cols])
            tail_r = dot(tail, spread_r[:, cols])
            value = v[0, span, cols].astype(F32)
            pulled_f = tail_f * dot(ins, doubled(grad_f))
            pulled_r = tail_r * dot(ins, doubled(grad_r))
            d_acts[span, cols] = d_v[0, span, cols] + pulled_f + pulled_r
            d_in = d_in + dot(spread_operand(tail_f * value), twice(stacked(grad_f), 1), COLS)
            d_in = d_in + dot(spread_operand(tail_r * value), twice(stacked(grad_r), 1), COLS)
            used = used + head_sums(pulled_f * value, sum_f[cols, :]) + head_sums(pulled_r * value, sum_r[cols, :])
            meet_f = jnp.sum(grad_f * state_f, axis=0, keepdims=True) * dx[0, b : b + 1, cols]
            meet_r = jnp.sum(grad_r * state_r, axis=0, keepdims=True) * dx[0, 2 + b : 3 + b, cols]
            zero = jnp.zeros((7, width), F32)
            decays = decays + head_sums(jnp.concatenate([meet_f, zero], axis=0), sum_f[cols, :])
            decays = decays + head_sums(jnp.concatenate([meet_r, zero], axis=0), sum_r[cols, :])
        d_acts[span, pl.ds(INNER, LANES)] = d_bc[0, span, :] + jnp.where(lane < STATE, d_in + swapped(d_in), 0.0)
        direct = sums[0, span, :] + used
        edge = decays[0:1] + jnp.sum(used, axis=0, keepdims=True)
        at_end = ((lane < HEADS) & (row == BLOCK - 1)) | ((lane >= HEADS) & (row == 0))
        grad = d_log[0, span, :] - used + jnp.where(at_end, edge, 0.0)
        grad = jnp.where(lane < HEADS, dot(upper, grad, precision=HIGHEST), dot(lower, grad, precision=HIGHEST))
        x = dt[0, span, :] + rates[0:1, :]
        step = softplus(x)
        sig = sigmoid(x)
        ratio = jnp.where(x < -17.0, 1.0, sig / step)
        d_x = direct * ratio - rates[1:2, :] * grad * sig
        d_x = jnp.where(lane < 2 * HEADS, d_x, 0.0)
        late[0, span, pl.ds(INNER + LANES, LANES)] = d_x.astype(BF16)
        d_small[0:1, :] += jnp.sum(d_x, axis=0, keepdims=True)
        d_small[1:2, :] -= rates[1:2, :] * jnp.sum(step * grad, axis=0, keepdims=True)
        if b == 0:
            beside(1, (1, 1))
            beside(2, (3, 0))
        else:
            beside(0, (0, 1))
            beside(1, (2, 0))
            beside(2, (3, 1))
    valid, masks = row_masks(info, m, (TOK_DEV, LANES))
    edge = jnp.zeros((HALO, LANES), F32)
    for chunk in range(PAIRS + 1):
        cols = pl.ds(chunk * LANES, LANES)
        source, own = (vals, cols) if chunk < PAIRS else (bc_in, pl.ds(0, LANES))
        windows = conv_windows(source, own)
        value = conv_value(windows, masks, taps, cols)
        sig = sigmoid(value)
        grad = valid * d_acts[:, cols] * (sig * (1.0 + value * (1.0 - sig)))
        total = jnp.zeros((HALO + TOK_DEV, LANES), F32)
        for k in range(CONV):
            masked = grad if k == 0 else grad * masks[k]
            d_taps[k : k + 1, cols] += jnp.sum(masked * windows[k], axis=0, keepdims=True)
            padded = jnp.concatenate([edge, masked, edge], axis=0)
            total = total + taps[k : k + 1, cols] * padded[k : k + HALO + TOK_DEV]
        d_taps[CONV : CONV + 1, cols] += jnp.sum(grad, axis=0, keepdims=True)
        before[0, :, cols] = total[:HALO]
        last[0, :, cols] = total[TOK_DEV:]
        late[0, :, cols] = total[HALO:].astype(BF16)
    beside(0, (1, 0))
    beside(1, (2, 1))
    beside(2, (4, 0), (4, 1), (5, 0), (5, 1))
    if levels:

        @pl.when(m == MB - 1)
        def _():
            first_out[...] = buffers[5][...].astype(F32)
            second_out[...] = buffers[11][...].astype(F32)


def once(shape):
    return pl.BlockSpec(shape, lambda *grid: (0,) * len(shape), pipeline_mode=pl.Buffered(1))


def per_micro(shape, column=0):
    return pl.BlockSpec((1,) + shape, lambda m, *rest: (m,) + (0,) * (len(shape) - 1) + (column,))


def per_block(width, column=0):
    return pl.BlockSpec((1, BLOCK, width), lambda m, b: (m, b, column))


def struct(*shape, dtype=F32):
    return jax.ShapeDtypeStruct(shape, dtype)


def call(kernel, grid, in_specs, out_specs, out_shape, scratch=(), flops=0, moved=0, identity=None):
    return pl.pallas_call(
        kernel,
        grid=grid,
        in_specs=in_specs,
        out_specs=out_specs,
        out_shape=out_shape,
        scratch_shapes=list(scratch),
        compiler_params=pltpu.CompilerParams(
            vmem_limit_bytes=VMEM_LIMIT, collective_id=identity, has_side_effects=identity is not None
        ),
        cost_estimate=pl.CostEstimate(flops=flops, bytes_accessed=moved, transcendentals=0),
    )


def shift(value, distance):
    count = lax.axis_size("dp")
    route = [(i, i + distance) for i in range(count) if 0 <= i + distance < count]
    return lax.ppermute(value, "dp", route)


def carry_steps(levels, up_row, down_row, gains, gains_other, gain_sems, up_in, down_in, up_out, down_out, buffers):
    up_other, down_other, up_chain, down_chain, up_sems, down_sems, up_link, down_link, out_sems = buffers
    me = lax.axis_index("dp")
    side = lax.rem(me, 2)
    level = me // 2
    partner = me + 1 - 2 * side
    above, below = me + 2, me - 2
    has_above, has_below = level < levels - 1, level > 0
    first = side == 0

    def remote(source, target, sems, k, device):
        return pltpu.make_async_remote_copy(
            src_ref=source, dst_ref=target, send_sem=sems.at[0, k], recv_sem=sems.at[1, k], device_id={"dp": device}
        )

    def swap_gains(m):
        return remote(gains.at[m], gains_other.at[m], gain_sems, m, partner)

    def swap_up(k):
        return remote(up_in.at[k], up_other.at[k], up_sems, k, partner)

    def swap_down(k):
        return remote(down_in.at[k], down_other.at[k], down_sems, k, partner)

    def climb(k):
        return remote(up_in.at[k], up_chain.at[k], up_link, k, above)

    def descend(k):
        return remote(down_in.at[k], down_chain.at[k], down_link, k, below)

    def keep_up(k):
        return pltpu.make_async_copy(up_other.at[k], up_out.at[k], out_sems.at[0, k])

    def keep_down(k):
        return pltpu.make_async_copy(down_other.at[k], down_out.at[k], out_sems.at[1, k])

    def greet(barrier):
        pl.semaphore_signal(barrier, inc=1, device_id={"dp": partner})

        @pl.when(has_above)
        def _():
            pl.semaphore_signal(barrier, inc=1, device_id={"dp": above})

        @pl.when(has_below)
        def _():
            pl.semaphore_signal(barrier, inc=1, device_id={"dp": below})

        return 1 + has_above.astype(jnp.int32) + has_below.astype(jnp.int32)

    def begin():
        @pl.when(level == 0)
        def _():
            up_chain[...] = jnp.zeros_like(up_chain)

        @pl.when(level == levels - 1)
        def _():
            down_chain[...] = jnp.zeros_like(down_chain)

    total = CHUNKS + LAG * (levels - 1)

    def places(step):
        return step - LAG * level, step - LAG * (levels - 1 - level)

    def send(low, high):
        @pl.loop(low, high)
        def _(k):
            @pl.when(k < CHUNKS)
            def _():
                swap_up(k).start()
                swap_down(k).start()

    def advance(step):
        up, down = places(step)

        @pl.when((up >= 0) & (up < CHUNKS))
        def _():
            swap_up(up).wait_recv()

            @pl.when(has_below)
            def _():
                climb(up).wait_recv()

            m = up // PARTS
            own, other = gains[m, up_row : up_row + 1], gains_other[m, up_row : up_row + 1]
            near, far = jnp.where(first, own, other), jnp.where(first, other, own)
            mine, theirs = up_in[up], up_other[up]
            before = up_chain[up]
            middle = jnp.where(first, mine, theirs) + near * before
            up_other[up] = jnp.where(first, before, middle)
            keep_up(up).start()

            @pl.when(has_above)
            def _():
                swap_up(up).wait_send()
                up_in[up] = jnp.where(first, theirs, mine) + far * middle
                climb(up).start()

        @pl.when((down >= 0) & (down < CHUNKS))
        def _():
            swap_down(down).wait_recv()

            @pl.when(has_above)
            def _():
                descend(down).wait_recv()

            m = down // PARTS
            own, other = gains[m, down_row : down_row + 1], gains_other[m, down_row : down_row + 1]
            near, far = jnp.where(first, other, own), jnp.where(first, own, other)
            mine, theirs = down_in[down], down_other[down]
            before = down_chain[down]
            middle = jnp.where(first, theirs, mine) + near * before
            down_other[down] = jnp.where(first, middle, before)
            keep_down(down).start()

            @pl.when(has_below)
            def _():
                swap_down(down).wait_send()
                down_in[down] = jnp.where(first, mine, theirs) + far * middle
                descend(down).start()

    def run(low, high, window):
        @pl.loop(low, high)
        def _(step):
            advance(step)
            if window:
                send(step + window, step + window + 1)

    def gains_here(m):
        swap_gains(m).wait_recv()

    def end(last):
        if last:

            @pl.loop(0, MB)
            def _(m):
                swap_gains(m).wait_send()

        @pl.loop(0, CHUNKS)
        def _(k):
            keep_up(k).wait()
            keep_down(k).wait()

            @pl.when(has_above)
            def _():
                climb(k).wait_send()

            @pl.when(jnp.logical_not(has_above))
            def _():
                swap_up(k).wait_send()

            @pl.when(has_below)
            def _():
                descend(k).wait_send()

            @pl.when(jnp.logical_not(has_below))
            def _():
                swap_down(k).wait_send()

    return greet, begin, lambda m: swap_gains(m).start(), gains_here, send, run, end, total


CARRY_SHAPE = (CHUNKS, STATE // PARTS, INNER)


def carry_buffers():
    return [pltpu.VMEM(CARRY_SHAPE, F32)] * 4 + [pltpu.SemaphoreType.DMA((2, CHUNKS))] * 5


def sum_steps(levels, parts, side_sems, level_sems):
    me = lax.axis_index("dp")
    side, level = lax.rem(me, 2), me // 2
    partner = me + 1 - 2 * side

    def level_at(d):
        return lax.rem(level + d + levels, levels)

    def device(d):
        return {"dp": 2 * level_at(d) + side}

    def remote(source, target, sems, k, where):
        return pltpu.make_async_remote_copy(
            src_ref=source, dst_ref=target, send_sem=sems.at[0, k], recv_sem=sems.at[1, k], device_id=where
        )

    def greet(barrier):
        pl.semaphore_signal(barrier, inc=1, device_id={"dp": partner})
        for d in range(1, levels):
            pl.semaphore_signal(barrier, inc=1, device_id=device(d))
        return levels

    def halve(i):
        return remote(parts[i][1], parts[i][2], side_sems, 2 * i, {"dp": partner})

    def join(i, theirs):
        full = parts[i][5]
        return remote(full.at[side], full.at[1 - side if theirs else side], side_sems, 2 * i + 1, {"dp": partner})

    def scatter(i, d, theirs):
        put, got = parts[i][3:5]
        return remote(put.at[level_at(d)], got.at[level_at(-d) if theirs else level], level_sems, 2 * i * levels + d, device(d))

    def gather(i, d, theirs):
        full = parts[i][5]
        target = full.at[side, level_at(-d) if theirs else level]
        return remote(full.at[side, level], target, level_sems, (2 * i + 1) * levels + d, device(d))

    def step_0(i):
        total, put = parts[i][:2]
        put[...] = total[1 - side].astype(BF16)
        halve(i).start()

    def step_1(i):
        total, _, got, put = parts[i][:4]
        halve(i).wait_recv()
        total[side] = total[side] + got[...].astype(F32)
        for d in range(1, levels):
            target = level_at(d)
            put[target] = total[side, target].astype(BF16)
            scatter(i, d, False).start()

    def step_2(i):
        total, _, _, _, got, full = parts[i]
        value = total[side, level]
        for d in range(1, levels):
            scatter(i, d, True).wait_recv()
            value = value + got[level_at(-d)].astype(F32)
        full[side, level] = value.astype(BF16)
        for d in range(1, levels):
            gather(i, d, False).start()

    def step_3(i):
        for d in range(1, levels):
            gather(i, d, True).wait_recv()
        join(i, False).start()

    def step_4(i):
        join(i, True).wait_recv()

    def close(i):
        halve(i).wait_send()
        join(i, False).wait_send()
        for d in range(1, levels):
            scatter(i, d, False).wait_send()
            gather(i, d, False).wait_send()

    return greet, (step_0, step_1, step_2, step_3, step_4, close)


def sum_buffers(levels, piece, width):
    low = pltpu.VMEM((levels, piece, width), BF16)
    both = (2, levels, piece, width)
    return [pltpu.VMEM(both, F32), low, low, low, low, pltpu.VMEM(both, BF16)]


def sum_semaphores(levels, count):
    return [pltpu.SemaphoreType.DMA((2, 2 * count)), pltpu.SemaphoreType.DMA((2, 2 * count * levels))]


PIECES = ((0, 512), (512, 512), (1024, 384), (1408, 384))


def total_kernel(
    levels, columns, info, hidden_t, late, d_gate, normed, w_all, w_back, x_in, cot_in, gain_in,
    gate_in, taps_in, scale_in, skip_in, small_in, selector,
    layer_out, tokens_out, inner_out, state_out, step_out, norm_out, taps_out, bias_out, steps_out, decay_out, skip_out, scale_out,
    third_in, norm_sum, mate_got, cross_put, cross_got, short_sum, short_got, short_sems, mate_sems, cross_sems, side_sems, level_sems, *buffers,
):
    me, part = lax.axis_index("dp"), lax.axis_index("fsdp")
    side, level = lax.rem(me, 2), me // 2
    core, column = lax.rem(part, 2), part // 2
    mate = part + 1 - 2 * core
    count = len(PIECES)
    parts = [buffers[6 * i : 6 * i + 6] for i in range(count)]
    greet, steps = sum_steps(levels, parts, side_sems, level_sems)

    def column_at(d):
        return lax.rem(column + d + columns, columns)

    def remote(source, target, sems, k, where):
        return pltpu.make_async_remote_copy(
            src_ref=source, dst_ref=target, send_sem=sems.at[0, k], recv_sem=sems.at[1, k], device_id=where
        )

    barrier = pltpu.get_barrier_semaphore()
    pl.semaphore_signal(barrier, inc=1, device_id={"fsdp": mate})
    for d in range(1, columns):
        pl.semaphore_signal(barrier, inc=1, device_id={"fsdp": 2 * column_at(d) + core})
    pl.semaphore_wait(barrier, greet(barrier) + columns)

    def to_mate(i, x):
        at = pl.ds(*PIECES[i])
        return remote(third_in.at[2 * x + 1 - core, :, at], mate_got.at[x, :, at], mate_sems, i * columns + x, {"fsdp": mate})

    def across(i, d, theirs):
        at = pl.ds(*PIECES[i])
        where = {"fsdp": 2 * column_at(d) + core}
        slot = column_at(-d) if theirs else column
        return remote(cross_put.at[column_at(d), :, at], cross_got.at[slot, :, at], cross_sems, i * columns + d, where)

    block_rows = third_in.shape[1]

    def third(owner, i):
        at = pl.ds(pl.multiple_of(owner * block_rows, 16), block_rows)
        cols = pl.ds(*PIECES[i])
        third_in[owner, :, cols] = dot(hidden_t[at, :], late[:, cols])

    def d_hidden_block(k):
        m, b = divmod(k, 2)
        at = slice(k * BLOCK, (k + 1) * BLOCK)
        grad = dot(d_gate[at], w_all[:, :INNER], COLS) + dot(late[at], w_all[:, INNER:], COLS)
        rows = x_in[at].astype(F32)
        scale = lax.rsqrt(jnp.mean(rows * rows, axis=1, keepdims=True) + EPSILON)
        norm_sum[...] += jnp.sum(grad * rows * scale, axis=0, keepdims=True)
        pulled = grad * gain_in[...]
        pull = (scale * scale * scale) * jnp.mean(rows * pulled, axis=1, keepdims=True)
        valid = row_masks(info, m, (BLOCK, D), b * BLOCK)[0]
        tokens_out[at] = scale * pulled - rows * pull + valid * cot_in[at].astype(F32)

    def layer_block(k):
        m, b = divmod(k, 2)
        at = slice(k * BLOCK, (k + 1) * BLOCK)
        branch = dot(normed[at], w_back[...])
        valid = row_masks(info, m, (BLOCK, D), b * BLOCK)[0]
        layer_out[at] = jnp.where(valid > 0.0, x_in[at].astype(F32) + branch, 0.0).astype(BF16)

    norm_sum[...] = jnp.zeros_like(norm_sum)
    for i in range(count):
        for x in range(columns):
            third(2 * x + 1 - core, i)
            to_mate(i, x).start()
    for i in range(count):
        for x in range(columns):
            third(2 * x + core, i)

    def cross(i):
        at = pl.ds(*PIECES[i])
        for x in range(columns):
            to_mate(i, x).wait_recv()
        for d in range(1, columns):
            x = column_at(d)
            cross_put[x, :, at] = (third_in[2 * x + core, :, at] + mate_got[x, :, at]).astype(BF16)
            across(i, d, False).start()

    cross(0)
    cross(1)
    for k in range(2 * MB - 2):
        d_hidden_block(k)

    lane = iota((8, LANES), 1)
    summed = jnp.where(lane < HEADS, head_sums(skip_in[...], selector[...]), 0.0)
    folded = small_in[...] + pltpu.roll(small_in[...], LANES - HEADS, axis=1)
    short_sum[0, 0:8, :] = taps_in[...]
    short_sum[0, 8:16, :] = jnp.zeros((8, CONV_COLS), F32)
    short_sum[0, 5:6, :INNER] = scale_in[0:1]
    short_sum[0, 8:9, :LANES] = small_in[0:1]
    short_sum[0, 9:10, :LANES] = folded[1:2]
    short_sum[0, 10:11, :LANES] = summed[0:1]
    routes = [{"fsdp": mate}, {"dp": me + 1 - 2 * side}]
    stride = 1
    while stride < columns:
        routes.append({"fsdp": part + 2 * stride - 4 * stride * lax.rem(column // stride, 2)})
        stride *= 2
    stride = 1
    while stride < levels:
        routes.append({"dp": me + 2 * stride - 4 * stride * lax.rem(level // stride, 2)})
        stride *= 2

    def short(k):
        return remote(short_sum.at[k], short_got.at[k], short_sems, k, routes[k])

    def short_step(k):
        if k > 0:
            short(k - 1).wait_recv()
            short_sum[k] = short_sum[k - 1] + short_got[k - 1]
        if k < len(routes):
            short(k).start()

    rows = parts[0][0].shape[2]

    def arrive(i):
        at = pl.ds(*PIECES[i])
        for d in range(1, columns):
            across(i, d, True).wait_recv()
        for x in range(2):
            for j in range(levels):
                here = pl.ds((x * levels + j) * rows, rows)
                value = third_in[part, here, at] + mate_got[column, here, at]
                for d in range(1, columns):
                    value = value + cross_got[column_at(-d), here, at].astype(F32)
                parts[i][0][x, j] = value
        steps[0](i)

    last = len(routes)
    for wave in range(count + 4):
        for stage in range(4, 0, -1):
            i = wave - stage
            if 0 <= i < count:
                steps[stage](i)
        if wave < count:
            arrive(wave)
        if wave + 2 < count:
            cross(wave + 2)
        if wave < 2:
            d_hidden_block(2 * MB - 2 + wave)
        elif wave < 2 + 2 * MB:
            layer_block(wave - 2)
        if wave == 1:
            short_sum[0, 6:7, :D] = norm_sum[...]
        if 1 <= wave <= last + 1:
            short_step(wave - 1)
    for k in range(count + 3, last + 1):
        short_step(k)

    result = short_sum.at[last]
    for f in range(2 * columns):

        @pl.when(part == f)
        def _():
            def own(row, rows, width, ref):
                size = width // (2 * columns)
                ref[...] = result[row : row + rows, f * size : (f + 1) * size]

            own(0, CONV, CONV_COLS, taps_out)
            own(4, 1, CONV_COLS, bias_out)
            own(5, 1, INNER, scale_out)
            own(6, 1, D, norm_out)
            own(8, 1, 2 * HEADS, steps_out)
            own(9, 1, HEADS, decay_out)
            own(10, 1, HEADS, skip_out)

    half = gate_in.shape[0] // 2
    for h in range(2):
        inner_out[:, h * D : (h + 1) * D] = gate_in[h * half : (h + 1) * half]
    for i in range(count):
        start, width = PIECES[i]
        for x in range(2):
            for j in range(levels):
                here = pl.ds((x * levels + j) * rows, rows)
                value = parts[i][5][x, j].astype(F32)
                inside = min(width, INNER - start)
                inner_out[here, INNER + start : INNER + start + inside] = value[:, :inside]
                if inside < width:
                    state_out[here, :] = value[:, inside : inside + LANES]
                    step_out[here, :] = value[:, inside + LANES : inside + LANES + 2 * HEADS]
    for i in range(count):
        steps[5](i)
        for x in range(columns):
            to_mate(i, x).wait_send()
        for d in range(1, columns):
            across(i, d, False).wait_send()
    for k in range(last):
        short(k).wait_send()


def total_fits(levels, shards, dp_count):
    rows = D // shards
    return dp_count == 2 * levels and shards % 2 == 0 and rows % (16 * levels) == 0 and 24 % shards == 0


def totals(operands, identity):
    dp_count, shards = lax.axis_size("dp"), lax.axis_size("fsdp")
    levels, columns = dp_count // 2, shards // 2
    rows = D // shards
    small = rows // levels // 2
    steps = (dp_count * shards).bit_length() - 1
    count = len(PIECES)

    def low(*shape):
        return pltpu.VMEM(shape, BF16)

    def full(*shape):
        return pltpu.VMEM(shape, F32)

    outs = pl.pallas_call(
        partial(total_kernel, levels, columns),
        in_specs=[SCALARS] + [pl.BlockSpec(memory_space=pltpu.VMEM)] * 15,
        out_specs=[pl.BlockSpec(memory_space=pltpu.VMEM)] * 12,
        out_shape=[struct(MB * TOK_DEV, D, dtype=BF16), struct(MB * TOK_DEV, D)]
        + [struct(rows, 2 * INNER), struct(rows, 2 * STATE), struct(rows, 2 * HEADS)]
        + [struct(1, D // shards), struct(CONV, CONV_COLS // shards), struct(1, CONV_COLS // shards)]
        + [struct(1, width // shards) for width in (2 * HEADS, HEADS, HEADS, INNER)],
        scratch_shapes=[full(shards, rows, LATE), full(1, D), full(columns, rows, LATE), low(columns, rows, LATE), low(columns, rows, LATE)]
        + [full(steps + 1, 16, CONV_COLS), full(steps, 16, CONV_COLS), pltpu.SemaphoreType.DMA((2, steps))]
        + [pltpu.SemaphoreType.DMA((2, count * columns))] * 2
        + sum_semaphores(levels, count)
        + [buffer for _, width in PIECES for buffer in sum_buffers(levels, small, width)],
        compiler_params=pltpu.CompilerParams(vmem_limit_bytes=VMEM_LIMIT, collective_id=identity, has_side_effects=True),
    )(*operands)
    heads = [out.reshape(MB, 1, TOK_DEV, D) for out in outs[:2]]
    flat = [out.reshape(-1) for out in outs[7:]]
    return heads + [outs[5].reshape(-1)] + list(outs[2:5]) + [outs[6]] + flat


def rms(values):
    return lax.rsqrt(jnp.mean(values * values, axis=-1, keepdims=True) + EPSILON)


def scatter_small(parts, shards):
    rows = []
    for part in parts:
        if part.ndim == 2:
            rows.append(part.reshape(part.shape[0], shards, -1).transpose(1, 0, 2).reshape(shards, -1))
        else:
            rows.append(part.reshape(shards, -1))
    flat = jnp.concatenate(rows, axis=1)
    size = flat.shape[1]
    padded = -(-size // LANES) * LANES
    return jnp.pad(flat, ((0, 0), (0, padded - size)))


def on_device(
    tokens, seq_lengths, norm_gain, w_inner, w_state, w_step, conv_weight, conv_bias, step_bias, decay_log, skip_gain, out_gain, w_out, cotangent,
):
    dp_count = lax.axis_size("dp")
    shards = lax.axis_size("fsdp")
    base = lax.axis_index("dp") * TOK_DEV
    lengths = seq_lengths[:, 0]
    info = jnp.concatenate([lengths.reshape(-1), jnp.stack([base, jnp.int32(dp_count * TOK_DEV)]).astype(jnp.int32)])
    width = 512

    def padded(part):
        return jnp.pad(part, ((0, 0),) * (part.ndim - 1) + ((0, width - part.shape[-1]),)).reshape(-1)

    small = [padded(part) for part in (conv_weight, conv_bias, out_gain, norm_gain, step_bias, decay_log, skip_gain)]
    mine = jnp.concatenate(small + [jnp.zeros((6 * width,), BF16)]).reshape(16, width)
    x, cot = tokens[:, 0], cotangent[:, 0]
    w_all, hidden, hidden_t, d_branch, d_branch_t, gain_in, taps, steps, skip, out_scale, spread_f, spread_r, sum_f, sum_r = gather_weights(
        info, x, cot, w_inner, w_state, w_step, mine, 4
    )
    rows = TOK_DEV + HALO
    zx = jnp.dot(hidden.reshape(MB * rows, D), w_all, preferred_element_type=F32).reshape(MB, rows, WIDE)

    levels = dp_count // 2
    zx_vals = per_micro((rows, INNER), 1)
    zx_bc = per_micro((rows, LANES), 2 * INNER // LANES)
    zx_dt = per_micro((rows, LANES), 2 * INNER // LANES + 1)
    taps_spec, steps_spec = once((8, CONV_COLS)), once((8, LANES))
    spread_spec, sum_spec = once((2 * LANES, INNER)), once((INNER, LANES))
    state_spec, dx_spec = per_micro((STATE, INNER)), per_micro((8, INNER))
    wide_spec, lane_spec = per_micro((TOK_DEV, INNER)), per_micro((TOK_DEV, LANES))
    row_spec, dx_all_spec, carry_spec = once((8, INNER)), once((MB, 8, INNER)), once(CARRY_SHAPE)

    def early(width, column):
        return pl.BlockSpec((1, rows, width), lambda s: (jnp.minimum(s, MB - 1), 0, column))

    def turning(s):
        return jnp.clip(s - MB, 0, 2 * MB - 1)

    def backing(s):
        return jnp.maximum(s - 3 * MB, 0)

    def block_at(pick, width):
        return pl.BlockSpec((1, BLOCK, width), lambda s: (pick(s) // 2, lax.rem(pick(s), 2), 0))

    back_spec = pl.BlockSpec((1, 1, STATE, INNER), lambda s: (turning(s) // 2, lax.rem(turning(s), 2), 0, 0))
    lanes_struct = struct(MB, TOK_DEV, LANES)
    lane_out, anywhere = block_at(backing, LANES), pl.BlockSpec(memory_space=pl.ANY)
    shard_rows = INNER // shards
    shard_spec = once((shard_rows, D))
    pairs = pltpu.SemaphoreType.DMA((2, shards // 2))
    block_scratch = pltpu.VMEM((BLOCK, INNER), F32)
    (
        v, bc, fr, frp, kept_f, kept_r, dx, normed, d_gate, back_f, back_r, d_out_gain, d_skip, d_v, d_bc, sums, d_log,
        first_grad, gate_grad, enter_f, enter_r, after_f, after_r, w_back,
    ) = call(
        partial(mixer_kernel, levels, shards // 2),
        (5 * MB,),
        [SCALARS, early(INNER, 1), early(LANES, 2 * INNER // LANES), early(LANES, 2 * INNER // LANES + 1), block_at(turning, INNER)]
        + [taps_spec, steps_spec, spread_spec, spread_spec, sum_spec, sum_spec, row_spec, row_spec]
        + [anywhere] * 4,
        [anywhere] * 9
        + [back_spec, back_spec]
        + [row_spec, row_spec, block_at(backing, INNER), lane_out, lane_out, lane_out, shard_spec, shard_spec]
        + [anywhere] * 5,
        [struct(MB, TOK_DEV, INNER, dtype=BF16)]
        + [lanes_struct] * 3
        + [struct(MB, STATE, INNER)] * 2
        + [struct(MB, 8, INNER)]
        + [struct(MB, TOK_DEV, INNER, dtype=BF16)] * 2
        + [struct(MB, 2, STATE, INNER)] * 2
        + [struct(8, INNER)] * 2
        + [struct(MB, TOK_DEV, INNER)]
        + [lanes_struct] * 3
        + [struct(shard_rows, D)] * 2
        + [struct(*CARRY_SHAPE)] * 4
        + [struct(INNER, D, dtype=BF16)],
        scratch=[pltpu.VMEM((MB, TOK_DEV, INNER), BF16)]
        + [pltpu.VMEM((MB, TOK_DEV, LANES), F32)] * 3
        + [pltpu.VMEM((MB, STATE, INNER), F32)] * 2
        + [pltpu.VMEM((MB, 8, INNER), F32)]
        + [pltpu.VMEM((MB, TOK_DEV, INNER), BF16)] * 2
        + [pltpu.VMEM((MB, TOK_DEV, D), BF16)]
        + [pltpu.VMEM((D, MB * TOK_DEV), BF16)] * 2
        + [pltpu.SemaphoreType.DMA((3,)), pltpu.SemaphoreType.DMA((7, MB)), pltpu.SemaphoreType.DMA((2, 2 * MB))]
        + [pltpu.VMEM((1, BLOCK, INNER), F32)] * 2
        + [block_scratch] * 5
        + [pltpu.VMEM((BLOCK, LANES), F32), pltpu.VMEM((2 * MB, BLOCK, INNER), BF16)]
        + [pltpu.VMEM((2 * MB, BLOCK, LANES), F32)] * 2
        + [pltpu.VMEM((INNER, D), BF16), pairs, pairs, pltpu.SemaphoreType.DMA((2,))]
        + shard_buffers(shards)
        + [pltpu.VMEM((MB, 8, INNER), F32), pltpu.SemaphoreType.DMA((2, MB))]
        + [pltpu.VMEM(CARRY_SHAPE, F32)] * 4
        + 2 * carry_buffers(),
        flops=50_000_000_000,
        moved=60_000_000,
        identity=0,
    )(
        info, zx, zx, zx, zx, taps, steps, spread_f, spread_r, sum_f, sum_r, skip, out_scale, w_out, d_branch, d_branch_t, hidden_t
    )

    def turned(grad):
        return grad.reshape(shard_rows, D // shard_rows, shard_rows).transpose(2, 1, 0).reshape(shard_rows, D)

    fits = total_fits(levels, shards, dp_count)
    if fits:
        split = (2, levels, shard_rows // (2 * levels), D)
        first_grad, gate_grad = first_grad.reshape(split), gate_grad.reshape(split)
    else:
        split = (8, LANES)
    unused = jnp.zeros((8, LANES), F32)
    chunk_spec = pl.BlockSpec((PARTS,) + CARRY_SHAPE[1:], lambda m: (m, 0, 0))
    late, before, last, d_taps, d_small, first_sum, gate_sum = call(
        partial(final_kernel, levels if fits else 0),
        (MB,),
        [SCALARS, zx_vals, zx_bc, zx_dt, taps_spec, steps_spec, wide_spec, lane_spec, lane_spec, lane_spec]
        + [chunk_spec, chunk_spec, state_spec, state_spec]
        + [dx_spec, chunk_spec, chunk_spec, per_micro((2, STATE, INNER)), per_micro((2, STATE, INNER))]
        + [wide_spec, lane_spec, lane_spec, lane_spec, spread_spec, spread_spec, sum_spec, sum_spec, once(split), once(split)],
        [per_micro((TOK_DEV, LATE)), per_micro((HALO, CONV_COLS)), per_micro((HALO, CONV_COLS)), once((8, CONV_COLS)), once((8, LANES)), once(split), once(split)],
        [
            struct(MB, TOK_DEV, LATE, dtype=BF16),
            struct(MB, HALO, CONV_COLS),
            struct(MB, HALO, CONV_COLS),
            struct(8, CONV_COLS),
            struct(8, LANES),
            struct(*split),
            struct(*split),
        ],
        scratch=[pltpu.VMEM((TOK_DEV, CONV_COLS), F32)]
        + (2 * sum_buffers(*split[1:]) + sum_semaphores(levels, 2) if fits else []),
        flops=2_000_000_000,
        moved=40_000_000,
        identity=3 if fits else None,
    )(
        info, zx, zx, zx, taps, steps, v, bc, fr, frp, enter_f, enter_r, kept_f, kept_r, dx, after_f, after_r, back_f, back_r,
        d_v, d_bc, sums, d_log, spread_f, spread_r, sum_f, sum_r, first_grad if fits else unused, gate_grad if fits else unused,
    )
    ending = (last + shift(before, -1)).astype(BF16)
    late = lax.dynamic_update_slice(late, ending, (0, TOK_DEV - HALO, 0)).reshape(MB * TOK_DEV, LATE)

    d_gate = d_gate.reshape(MB * TOK_DEV, INNER)
    normed = normed.reshape(MB * TOK_DEV, INNER)
    if fits:
        flat = [part.reshape(MB * TOK_DEV, D) for part in (x, cot)]
        grads = totals(
            (info, hidden_t, late, d_gate, normed, w_all, w_back, *flat, gain_in, gate_sum.reshape(shard_rows, D))
            + (d_taps, d_out_gain, d_skip, d_small, sum_f),
            2,
        )
        return (*grads, turned(first_sum))

    def owned(grad):
        return lax.psum_scatter(grad, "fsdp", scatter_dimension=0, tiled=True)

    places = base + jnp.arange(TOK_DEV, dtype=jnp.int32)
    first = lengths[:, :1]
    start = (first + BLOCK - 1) // BLOCK * BLOCK
    valid = (places[None] < first) | (places[None] >= start) & (places[None] < start + lengths[:, 1:])
    valid = valid[..., None]
    branch = dot(normed, w_back).reshape(MB, TOK_DEV, D)
    x_rows = x.astype(F32)
    layer_out = jnp.where(valid, x_rows + branch, 0.0).astype(BF16)
    late_grad = dot(hidden_t, late)
    d_hidden = dot(d_gate, w_all[:, :INNER], COLS) + dot(late, w_all[:, INNER:], COLS)
    d_hidden = d_hidden.reshape(MB, TOK_DEV, D)
    scale = rms(x_rows)
    d_norm_gain = jnp.sum(d_hidden * x_rows * scale, axis=(0, 1))
    pulled = d_hidden * gain_in
    d_x = scale * pulled - x_rows * (scale * scale * scale) * jnp.mean(x_rows * pulled, axis=-1, keepdims=True)
    tokens_grad = d_x + jnp.where(valid, cot.astype(F32), 0.0)
    d_skip_gain = jnp.sum(d_skip[0].reshape(HEADS, HEAD_DIM), axis=1)
    d_decay = d_small[1, :HEADS] + d_small[1, HEADS : 2 * HEADS]
    small = (d_norm_gain, d_taps[:CONV], d_taps[CONV], d_small[0, : 2 * HEADS], d_decay, d_skip_gain, d_out_gain[0])
    w_out_grad, gate_grad, late_grad = lax.psum((first_grad, gate_grad, owned(late_grad)), "dp")
    summed = lax.psum(scatter_small(small, shards), ("dp", "fsdp"))
    own = lax.dynamic_slice_in_dim(summed, lax.axis_index("fsdp"), 1, axis=0)[0]
    pieces = []
    at = 0
    for part in (norm_gain, conv_weight, conv_bias, step_bias, decay_log, skip_gain, out_gain):
        pieces.append(own[at : at + part.size].reshape(part.shape))
        at += part.size
    gate_grad = jnp.concatenate([gate_grad[: shard_rows // 2], gate_grad[shard_rows // 2 :]], axis=1)
    w_inner_grad = jnp.concatenate([gate_grad, late_grad[:, :INNER]], axis=1)
    w_state_grad = late_grad[:, INNER : INNER + 2 * STATE]
    w_step_grad = late_grad[:, INNER + LANES : INNER + LANES + 2 * HEADS]
    grads = pieces[:1] + [w_inner_grad, w_state_grad, w_step_grad] + pieces[1:] + [turned(w_out_grad)]
    return (layer_out[:, None], tokens_grad[:, None], *grads)


def solution(mesh):
    rows, vector, matrix = P(None, "fsdp", "dp", None), P("fsdp"), P("fsdp", None)
    weights = (vector, matrix, matrix, matrix, P(None, "fsdp"), vector, vector, vector, vector, vector, matrix)
    return jax.shard_map(
        on_device,
        mesh=mesh,
        in_specs=(rows, P(None, "fsdp", None)) + weights + (rows,),
        out_specs=(rows, rows) + weights,
        check_vma=False,
    )
```

profile of v0, /device:TPU:0, one launch (start us, length us, event | category | flops | bytes accessed | tf_op | source)
XLA Modules:
  0.0 338.9 jit_solution(14268297094166128827)
XLA Ops:
  0.6 0.7 pad.30
  1.3 0.7 pad.28
  2.0 0.7 pad.31
  2.7 0.7 pad.32
  3.3 0.7 pad.33
  4.0 0.7 pad.29
  4.7 0.8 copy.33
  5.5 0.7 pad_bitcast_fusion
  7.5 0.6 reshape.85.mine
  8.1 1.5 copy.34.w_step
  9.6 0.6 pad_add_fusion.info
  10.2 33.9 %shard_map.237 = (bf16[768,3328]{1,0:T(8,128)(2,1)}, bf16[3,264,768]{2,1,0:T(8,128)(2,1)}, bf16[768,768]{1,0:T(8,128)(2,1)}, bf16[3,256,768]{2,1,0:T(8,128)(2,1)...) custom-call(s32[8]{0:T(128)} %pad_add_fusion.info, ...), custom_call_target="tpu_custom_call" | custom-call | tf_op jit(solution)/shard_map/pallas_call | solution.py:324
  44.1 11.1 %fusion.vals.bc_in.dt.gate = f32[3,264,3328]{2,1,0:T(8,128)} fusion(bf16[3,264,768]{2,1,0:T(8,128)(2,1)} %get-tuple-element.71, bf16[768,3328]{1,0:T(8,128)(2,1)} %get-tuple-element.72.w_all), kind=kOutput, calls=%fused_computation | convolution fusion | flops 4048551936 | bytes 16871424 | tf_op jit(solution)/shard_map/dot_general | solution.py:1555
  55.1 152.2 %shard_map.238 = (bf16[3,256,1536]{2,1,0:T(8,128)(2,1)}, f32[3,256,128]{2,1,0:T(8,128)}, f32[3,256,128]{2,1,0:T(8,128)}, f32[3,256,128]{2,1,0:T(8,128)}, f32[3,6...) custom-call(s32[8]{0:T(128)} %pad_add_fusion.info, ...), custom_call_target="tpu_custom_call" | custom-call | flops 49999998976 | bytes 60000000 | tf_op jit(solution)/shard_map/pallas_call | solution.py:1589
  207.4 50.5 %shard_map.239 = (bf16[3,256,1792]{2,1,0:T(8,128)(2,1)}, f32[3,8,1664]{2,1,0:T(8,128)}, f32[3,8,1664]{2,1,0:T(8,128)}, f32[8,1664]{1,0:T(8,128)}, f32[8,128]{1,0...) custom-call(s32[8]{0:T(128)} %pad_add_fusion.info, f32[3,264,3328]{2,1,0:T(8,128)} %fusion.vals.bc_in.dt.gate, ...), custom_call_target="tpu_custom_call" | custom-call | flops 2000000000 | bytes 40000000 | tf_op jit(solution)/shard_map/pallas_call | solution.py:1646
  257.9 1.3 collective-permute-start
  259.2 1.9 reshape.100
  261.1 1.2 copy.35
  262.4 1.1 copy.40
  263.5 1.8 collective-permute-done
  265.3 0.7 fusion.2
  266.0 60.0 %shard_map.240 = (bf16[768,768]{1,0:T(8,128)(2,1)}, f32[768,768]{1,0:T(8,128)}, f32[192,3072]{1,0:T(8,128)}, f32[192,128]{1,0:T(8,128)}, f32[192,48]{1,0:T(8,128...) custom-call(s32[8]{0:T(128)} %pad_add_fusion.info, ...), custom_call_target="tpu_custom_call" | custom-call | tf_op jit(solution)/shard_map/pallas_call | solution.py:1498
  326.0 1.6 copy.38
  327.6 1.4 reduce
  329.0 2.4 copy.59
  331.4 1.4 copy.60
  332.8 0.6 copy.61
  333.3 0.5 copy-done
  333.9 1.4 copy.62
  335.3 0.6 copy.63
  336.0 0.6 copy.64
  336.6 0.6 copy.65
  (32 shorter events, 3.0 us)
Async XLA Ops:
  257.9 7.4 %collective-permute-start = (f32[3,8,1664]{2,1,0:T(8,128)}, f32[3,8,1664]{2,1,0:T(8,128)S(1)}, u32[]{:S(2)}, u32[]{:S(2)}) collective-permute-start(f32[3,8,1664]{2,1,0:T(8,128)} %get-tuple-element.104), channel_id=1, source_target_pairs={{4,0},{8,4},{12,8},{16,12},{20,16},{24,20},{28,24},{5,1},{9,5},{13... | collective-permute-start | bytes 479240 | tf_op jit(solution)/shard_map/ppermute | solution.py:1022
  262.4 2.9 copy-start.2
  327.6 3.8 %copy-start.1 = (f32[768,768]{1,0:T(8,128)S(1)}, f32[768,768]{1,0:T(8,128)}, u32[]{:S(2)}) copy-start(f32[768,768]{1,0:T(8,128)} %get-tuple-element.115) | copy-start | bytes 7077892
  331.4 1.4 copy-start.6
  331.4 2.5 copy-start
  333.9 1.4 copy-start.3
  333.9 2.1 copy-start.4
  333.9 2.7 copy-start.5
  333.9 3.3 copy-start.9
  333.9 3.8 %copy-start.8 = (f32[1,6]{1,0:T(1,128)S(1)}, f32[1,6]{1,0:T(1,128)}, u32[]{:S(2)}) copy-start(f32[1,6]{1,0:T(1,128)} %get-tuple-element.123) | copy-start | bytes 76
  333.9 4.3 %copy-start.7 = (f32[1,6]{1,0:T(1,128)S(1)}, f32[1,6]{1,0:T(1,128)}, u32[]{:S(2)}) copy-start(f32[1,6]{1,0:T(1,128)} %get-tuple-element.124) | copy-start | bytes 76
where the time goes:
time: 340 us; the launch traced here: 339 us
  Pallas kernels  297 us (87%)
  local copies, waits for them, and re-layouts  24.5 us (7%)
  matrix products  11.1 us (3%)
    pallas_call x1, Pallas kernels, on_device(): call(partial(mixer_kernel, levels, shards // 2), (5 * MB,), [SCALARS, ear...  152 us
    pallas_call x1, Pallas kernels, totals(): pl.pallas_call(partial(total_kernel, levels, columns), in_specs=[SCALARS]...  60 us
    pallas_call x1, Pallas kernels, on_device(): call(partial(final_kernel, levels if fits else 0), (MB,), [SCALARS, zx_va...  50.5 us
    pallas_call x1, Pallas kernels, gather_weights(): pl.pallas_call(partial(gather_kernel, count, columns), in_specs=[SCALARS]...  33.9 us
    unnamed x43, local copies, waits for them, and re-layouts  16.6 us
    dot_general x1, matrix products, on_device(): jnp.dot(hidden.reshape(MB * rows, D), w_all, preferred_element_type=F32)  11.1 us
  transfers between devices with their start and end apart: 1, of which 1 were waited for; matrix products, arithmetic and copies ran while one was open for 1% of the time, Pallas kernels for 0%

commit v1 on v0

--- a/solution.py
+++ b/solution.py
@@ -238,17 +238,23 @@
         small_copy(d, True).wait_recv()
     small[part] = mine[...]
     wide, heads = CONV_COLS // shards, HEADS // shards
-    for f in range(shards):
-        value = small[f].astype(F32)
-        taps[: CONV + 1, f * wide : (f + 1) * wide] = value[: CONV + 1, :wide]
-        gain = value[5:6, : INNER // shards]
-        scale[:, f * INNER // shards : (f + 1) * INNER // shards] = jnp.broadcast_to(gain, (8, INNER // shards))
-        norm[:, f * rows : (f + 1) * rows] = value[6:7, :rows]
-        steps[0:1, 2 * f * heads : 2 * (f + 1) * heads] = value[7:8, : 2 * heads]
-        rates = jnp.exp(value[8:9, :heads])
-        steps[1:2, f * heads : (f + 1) * heads] = rates
-        steps[1:2, HEADS + f * heads : HEADS + (f + 1) * heads] = rates
-        skip_row[0:1, f * heads : (f + 1) * heads] = value[9:10, :heads]
+    at = 0
+    fields = [(taps, k, 1, wide) for k in range(CONV + 1)] + [(scale, 0, 8, INNER // shards), (norm, 0, 1, rows)]
+    fields += [(steps, 0, 1, 2 * heads), (steps, 1, 1, heads), (skip_row, 0, 1, heads)]
+    for ref, row, height, width in fields:
+        done = 0
+        while done < width:
+            line, lane = divmod(at + done, LANES)
+            size = min(width - done, LANES - lane)
+            for f in range(shards):
+                value = small[f, line : line + 1, lane : lane + size].astype(F32)
+                if ref is steps and row == 1:
+                    value = jnp.exp(value)
+                    ref[row : row + 1, HEADS + f * width + done : HEADS + f * width + done + size] = value
+                value = jnp.broadcast_to(value, (height, size))
+                ref[row : row + height, f * width + done : f * width + done + size] = value
+            done += size
+        at += width
     skip[...] = dot(spread_operand(skip_row[...]), spread_f[...])
 
     @pl.when(has_last)
@@ -862,12 +868,23 @@
 def final_kernel(
     levels, info, vals, bc_in, dt, taps, rates, v, bc, fr, frp, enter_f, enter_r, kept_f, kept_r, dx, after_f, after_r, back_f, back_r,
     d_v, d_bc, sums, d_log, spread_f, spread_r, sum_f, sum_r, first_in, second_in,
-    late, before, last, d_taps, d_small, first_out, second_out, d_acts, *buffers,
+    late, before, last, ending, d_taps, d_small, first_out, second_out, d_acts, *buffers,
 ):
     m = pl.program_id(0)
     forward, reverse = keeps(info, m)
     if levels:
-        greet, steps = sum_steps(levels, (buffers[:6], buffers[6:12]), *buffers[12:])
+        greet, steps = sum_steps(levels, (buffers[:6], buffers[6:12]), *buffers[12:14])
+        leaving, arriving, kept, edge_sems = buffers[14:]
+        me = lax.axis_index("dp")
+        side = lax.rem(me, 2)
+        neighbour = me - 1 + 2 * side
+        paired = (neighbour >= 0) & (neighbour < 2 * levels)
+
+        def edge_copy(k):
+            return pltpu.make_async_remote_copy(
+                src_ref=leaving.at[k], dst_ref=arriving.at[k], send_sem=edge_sems.at[0, k], recv_sem=edge_sems.at[1, k],
+                device_id={"dp": me - 1},
+            )
 
     def beside(at, *todo):
         if levels:
@@ -882,7 +899,17 @@
         @pl.when(m == 0)
         def _():
             barrier = pltpu.get_barrier_semaphore()
-            pl.semaphore_wait(barrier, greet(barrier))
+
+            @pl.when(paired)
+            def _():
+                pl.semaphore_signal(barrier, inc=1, device_id={"dp": neighbour})
+
+            pl.semaphore_wait(barrier, greet(barrier) + paired.astype(jnp.int32))
+
+            @pl.when(me == 2 * levels - 1)
+            def _():
+                arriving[...] = jnp.zeros_like(arriving)
+
             buffers[0][...] = first_in[...]
             buffers[6][...] = second_in[...]
 
@@ -950,11 +977,9 @@
         d_small[1:2, :] -= rates[1:2, :] * jnp.sum(step * grad, axis=0, keepdims=True)
         if b == 0:
             beside(1, (1, 1))
-            beside(2, (3, 0))
         else:
             beside(0, (0, 1))
             beside(1, (2, 0))
-            beside(2, (3, 1))
     valid, masks = row_masks(info, m, (TOK_DEV, LANES))
     edge = jnp.zeros((HALO, LANES), F32)
     for chunk in range(PAIRS + 1):
@@ -973,16 +998,36 @@
         d_taps[CONV : CONV + 1, cols] += jnp.sum(grad, axis=0, keepdims=True)
         before[0, :, cols] = total[:HALO]
         last[0, :, cols] = total[TOK_DEV:]
+        if levels:
+            leaving[m, :, cols] = total[:HALO]
+            kept[m, :, cols] = total[TOK_DEV:]
         late[0, :, cols] = total[HALO:].astype(BF16)
     beside(0, (1, 0))
     beside(1, (2, 1))
-    beside(2, (4, 0), (4, 1), (5, 0), (5, 1))
     if levels:
+
+        @pl.when(me > 0)
+        def _():
+            edge_copy(m).start()
 
         @pl.when(m == MB - 1)
         def _():
-            first_out[...] = buffers[5][...].astype(F32)
-            second_out[...] = buffers[11][...].astype(F32)
+            for i, out in ((0, first_out), (1, second_out)):
+                steps[3](i, False)
+                out[...] = buffers[6 * i + 5][side]
+            for i in range(2):
+                steps[5](i, False)
+            for k in range(MB):
+
+                @pl.when(me < 2 * levels - 1)
+                def _():
+                    edge_copy(k).wait_recv()
+
+                ending[k] = kept[k] + arriving[k]
+
+                @pl.when(me > 0)
+                def _():
+                    edge_copy(k).wait_send()
 
 
 def once(shape):
@@ -1252,17 +1297,19 @@
         for d in range(1, levels):
             gather(i, d, False).start()
 
-    def step_3(i):
+    def step_3(i, joined=True):
         for d in range(1, levels):
             gather(i, d, True).wait_recv()
-        join(i, False).start()
+        if joined:
+            join(i, False).start()
 
     def step_4(i):
         join(i, True).wait_recv()
 
-    def close(i):
+    def close(i, joined=True):
         halve(i).wait_send()
-        join(i, False).wait_send()
+        if joined:
+            join(i, False).wait_send()
         for d in range(1, levels):
             scatter(i, d, False).wait_send()
             gather(i, d, False).wait_send()
@@ -1284,9 +1331,10 @@
 
 
 def total_kernel(
-    levels, columns, info, hidden_t, late, d_gate, normed, w_all, w_back, x_in, cot_in, gain_in,
-    gate_in, taps_in, scale_in, skip_in, small_in, selector,
-    layer_out, tokens_out, inner_out, state_out, step_out, norm_out, taps_out, bias_out, steps_out, decay_out, skip_out, scale_out,
+    levels, columns, info, hidden_t_in, late_in, w_all_in, d_gate_in, x_hbm, cot_hbm, w_back_in, normed_in, gain_in,
+    first_in, gate_in, ending, taps_in, scale_in, skip_in, small_in, selector,
+    layer_hbm, tokens_hbm, first_out, inner_out, state_out, step_out, norm_out, taps_out, bias_out, steps_out, decay_out, skip_out, scale_out,
+    hidden_t, late, w_all, d_gate, x_in, cot_in, w_back, normed, layer_out, tokens_out, first_sum, first_full, gate_full, load_sems, keep_sems, join_sems,
     third_in, norm_sum, mate_got, cross_put, cross_got, short_sum, short_got, short_sems, mate_sems, cross_sems, side_sems, level_sems, *buffers,
 ):
     me, part = lax.axis_index("dp"), lax.axis_index("fsdp")
@@ -1295,6 +1343,19 @@
     mate = part + 1 - 2 * core
     count = len(PIECES)
     parts = [buffers[6 * i : 6 * i + 6] for i in range(count)]
+    sources = (hidden_t_in, late_in, w_all_in, d_gate_in, x_hbm, cot_hbm, w_back_in, normed_in)
+    places = (hidden_t, late, w_all, d_gate, x_in, cot_in, w_back, normed)
+
+    def load(i):
+        return pltpu.make_async_copy(sources[i], places[i], load_sems.at[i])
+
+    def keep(i, k):
+        ref, out = ((layer_out, layer_hbm), (tokens_out, tokens_hbm))[i]
+        at = pl.ds(k * BLOCK, BLOCK)
+        return pltpu.make_async_copy(ref.at[at], out.at[at], keep_sems.at[i, k])
+
+    for i in range(len(sources)):
+        load(i).start()
     greet, steps = sum_steps(levels, parts, side_sems, level_sems)
 
     def column_at(d):
@@ -1320,6 +1381,20 @@
         where = {"fsdp": 2 * column_at(d) + core}
         slot = column_at(-d) if theirs else column
         return remote(cross_put.at[column_at(d), :, at], cross_got.at[slot, :, at], cross_sems, i * columns + d, where)
+
+    joins = (first_full, gate_full)
+
+    def join(i, theirs):
+        full = joins[i]
+        return remote(full.at[side], full.at[1 - side if theirs else side], join_sems, i, {"dp": me + 1 - 2 * side})
+
+    for i, ref in enumerate((first_in, gate_in)):
+        joins[i][side] = ref[...]
+        join(i, False).start()
+    load(0).wait()
+    load(1).wait()
+    for m in range(MB):
+        late[(m + 1) * TOK_DEV - HALO : (m + 1) * TOK_DEV, :CONV_COLS] = ending[m].astype(BF16)
 
     block_rows = third_in.shape[1]
 
@@ -1339,6 +1414,7 @@
         pull = (scale * scale * scale) * jnp.mean(rows * pulled, axis=1, keepdims=True)
         valid = row_masks(info, m, (BLOCK, D), b * BLOCK)[0]
         tokens_out[at] = scale * pulled - rows * pull + valid * cot_in[at].astype(F32)
+        keep(1, k).start()
 
     def layer_block(k):
         m, b = divmod(k, 2)
@@ -1346,6 +1422,7 @@
         branch = dot(normed[at], w_back[...])
         valid = row_masks(info, m, (BLOCK, D), b * BLOCK)[0]
         layer_out[at] = jnp.where(valid > 0.0, x_in[at].astype(F32) + branch, 0.0).astype(BF16)
+        keep(0, k).start()
 
     norm_sum[...] = jnp.zeros_like(norm_sum)
     for i in range(count):
@@ -1367,6 +1444,8 @@
 
     cross(0)
     cross(1)
+    for i in range(2, 6):
+        load(i).wait()
     for k in range(2 * MB - 2):
         d_hidden_block(k)
 
@@ -1427,6 +1506,9 @@
         if wave < 2:
             d_hidden_block(2 * MB - 2 + wave)
         elif wave < 2 + 2 * MB:
+            if wave == 2:
+                load(6).wait()
+                load(7).wait()
             layer_block(wave - 2)
         if wave == 1:
             short_sum[0, 6:7, :D] = norm_sum[...]
@@ -1452,9 +1534,18 @@
             own(9, 1, HEADS, decay_out)
             own(10, 1, HEADS, skip_out)
 
-    half = gate_in.shape[0] // 2
+    for i in range(2):
+        join(i, True).wait_recv()
+    tall = gate_in.shape[1]
     for h in range(2):
-        inner_out[:, h * D : (h + 1) * D] = gate_in[h * half : (h + 1) * half]
+        for j in range(levels):
+            inner_out[j * tall : (j + 1) * tall, h * D : (h + 1) * D] = gate_full[h, j].astype(F32)
+            at = (h * levels + j) * tall
+            first_sum[at : at + tall] = first_full[h, j].astype(F32)
+    tall = first_sum.shape[0]
+    for g in range(D // tall):
+        at = slice(g * tall, (g + 1) * tall)
+        first_out[:, at] = jnp.transpose(first_sum[:, at])
     for i in range(count):
         start, width = PIECES[i]
         for x in range(2):
@@ -1474,11 +1565,15 @@
             across(i, d, False).wait_send()
     for k in range(last):
         short(k).wait_send()
+    for i in range(2):
+        join(i, False).wait_send()
+        for k in range(2 * MB):
+            keep(i, k).wait()
 
 
 def total_fits(levels, shards, dp_count):
     rows = D // shards
-    return dp_count == 2 * levels and shards % 2 == 0 and rows % (16 * levels) == 0 and 24 % shards == 0
+    return dp_count == 2 * levels and shards % 2 == 0 and rows % (16 * levels) == 0 and 2 * rows % LANES == 0 and 24 % shards == 0
 
 
 def totals(operands, identity):
@@ -1497,13 +1592,16 @@
 
     outs = pl.pallas_call(
         partial(total_kernel, levels, columns),
-        in_specs=[SCALARS] + [pl.BlockSpec(memory_space=pltpu.VMEM)] * 15,
-        out_specs=[pl.BlockSpec(memory_space=pltpu.VMEM)] * 12,
-        out_shape=[struct(MB * TOK_DEV, D, dtype=BF16), struct(MB * TOK_DEV, D)]
+        in_specs=[SCALARS] + [pl.BlockSpec(memory_space=pl.ANY)] * 8 + [pl.BlockSpec(memory_space=pltpu.VMEM)] * 9,
+        out_specs=[pl.BlockSpec(memory_space=pl.ANY)] * 2 + [pl.BlockSpec(memory_space=pltpu.VMEM)] * 11,
+        out_shape=[struct(MB * TOK_DEV, D, dtype=BF16), struct(MB * TOK_DEV, D), struct(2 * rows, D)]
         + [struct(rows, 2 * INNER), struct(rows, 2 * STATE), struct(rows, 2 * HEADS)]
         + [struct(1, D // shards), struct(CONV, CONV_COLS // shards), struct(1, CONV_COLS // shards)]
         + [struct(1, width // shards) for width in (2 * HEADS, HEADS, HEADS, INNER)],
-        scratch_shapes=[full(shards, rows, LATE), full(1, D), full(columns, rows, LATE), low(columns, rows, LATE), low(columns, rows, LATE)]
+        scratch_shapes=[pltpu.VMEM(operand.shape, BF16) for operand in operands[1:9]]
+        + [low(MB * TOK_DEV, D), full(MB * TOK_DEV, D), full(2 * rows, D), low(2, levels, small * 2, D), low(2, levels, small * 2, D)]
+        + [pltpu.SemaphoreType.DMA((8,)), pltpu.SemaphoreType.DMA((2, 2 * MB)), pltpu.SemaphoreType.DMA((2, 2))]
+        + [full(shards, rows, LATE), full(1, D), full(columns, rows, LATE), low(columns, rows, LATE), low(columns, rows, LATE)]
         + [full(steps + 1, 16, CONV_COLS), full(steps, 16, CONV_COLS), pltpu.SemaphoreType.DMA((2, steps))]
         + [pltpu.SemaphoreType.DMA((2, count * columns))] * 2
         + sum_semaphores(levels, count)
@@ -1511,8 +1609,8 @@
         compiler_params=pltpu.CompilerParams(vmem_limit_bytes=VMEM_LIMIT, collective_id=identity, has_side_effects=True),
     )(*operands)
     heads = [out.reshape(MB, 1, TOK_DEV, D) for out in outs[:2]]
-    flat = [out.reshape(-1) for out in outs[7:]]
-    return heads + [outs[5].reshape(-1)] + list(outs[2:5]) + [outs[6]] + flat
+    flat = [out.reshape(-1) for out in outs[8:]]
+    return heads + [outs[6].reshape(-1)] + list(outs[3:6]) + [outs[7]] + flat, outs[2]
 
 
 def rms(values):
@@ -1540,13 +1638,9 @@
     base = lax.axis_index("dp") * TOK_DEV
     lengths = seq_lengths[:, 0]
     info = jnp.concatenate([lengths.reshape(-1), jnp.stack([base, jnp.int32(dp_count * TOK_DEV)]).astype(jnp.int32)])
-    width = 512
-
-    def padded(part):
-        return jnp.pad(part, ((0, 0),) * (part.ndim - 1) + ((0, width - part.shape[-1]),)).reshape(-1)
-
-    small = [padded(part) for part in (conv_weight, conv_bias, out_gain, norm_gain, step_bias, decay_log, skip_gain)]
-    mine = jnp.concatenate(small + [jnp.zeros((6 * width,), BF16)]).reshape(16, width)
+    small = [part.reshape(-1) for part in (conv_weight, conv_bias, out_gain, norm_gain, step_bias, decay_log, skip_gain)]
+    flat = jnp.concatenate(small)
+    mine = jnp.pad(flat, (0, 32 * LANES - flat.shape[0])).reshape(32, LANES)
     x, cot = tokens[:, 0], cotangent[:, 0]
     w_all, hidden, hidden_t, d_branch, d_branch_t, gain_in, taps, steps, skip, out_scale, spread_f, spread_r, sum_f, sum_r = gather_weights(
         info, x, cot, w_inner, w_state, w_step, mine, 4
@@ -1640,28 +1734,31 @@
         split = (2, levels, shard_rows // (2 * levels), D)
         first_grad, gate_grad = first_grad.reshape(split), gate_grad.reshape(split)
     else:
-        split = (8, LANES)
-    unused = jnp.zeros((8, LANES), F32)
+        split = (1, 16, LANES)
+    unused = jnp.zeros(split, F32)
+    edge_buffers = [pltpu.VMEM((MB, HALO, CONV_COLS), F32)] * 3 + [pltpu.SemaphoreType.DMA((2, MB))]
     chunk_spec = pl.BlockSpec((PARTS,) + CARRY_SHAPE[1:], lambda m: (m, 0, 0))
-    late, before, last, d_taps, d_small, first_sum, gate_sum = call(
+    late, before, last, ending, d_taps, d_small, first_sum, gate_sum = call(
         partial(final_kernel, levels if fits else 0),
         (MB,),
         [SCALARS, zx_vals, zx_bc, zx_dt, taps_spec, steps_spec, wide_spec, lane_spec, lane_spec, lane_spec]
         + [chunk_spec, chunk_spec, state_spec, state_spec]
         + [dx_spec, chunk_spec, chunk_spec, per_micro((2, STATE, INNER)), per_micro((2, STATE, INNER))]
         + [wide_spec, lane_spec, lane_spec, lane_spec, spread_spec, spread_spec, sum_spec, sum_spec, once(split), once(split)],
-        [per_micro((TOK_DEV, LATE)), per_micro((HALO, CONV_COLS)), per_micro((HALO, CONV_COLS)), once((8, CONV_COLS)), once((8, LANES)), once(split), once(split)],
+        [per_micro((TOK_DEV, LATE)), per_micro((HALO, CONV_COLS)), per_micro((HALO, CONV_COLS)), once((MB, HALO, CONV_COLS)), once((8, CONV_COLS)), once((8, LANES))]
+        + [once(split[1:])] * 2,
         [
             struct(MB, TOK_DEV, LATE, dtype=BF16),
             struct(MB, HALO, CONV_COLS),
             struct(MB, HALO, CONV_COLS),
+            struct(MB, HALO, CONV_COLS),
             struct(8, CONV_COLS),
             struct(8, LANES),
-            struct(*split),
-            struct(*split),
+            struct(*split[1:], dtype=BF16),
+            struct(*split[1:], dtype=BF16),
         ],
         scratch=[pltpu.VMEM((TOK_DEV, CONV_COLS), F32)]
-        + (2 * sum_buffers(*split[1:]) + sum_semaphores(levels, 2) if fits else []),
+        + (2 * sum_buffers(*split[1:]) + sum_semaphores(levels, 2) + edge_buffers if fits else []),
         flops=2_000_000_000,
         moved=40_000_000,
         identity=3 if fits else None,
@@ -1669,19 +1766,20 @@
         info, zx, zx, zx, taps, steps, v, bc, fr, frp, enter_f, enter_r, kept_f, kept_r, dx, after_f, after_r, back_f, back_r,
         d_v, d_bc, sums, d_log, spread_f, spread_r, sum_f, sum_r, first_grad if fits else unused, gate_grad if fits else unused,
     )
-    ending = (last + shift(before, -1)).astype(BF16)
-    late = lax.dynamic_update_slice(late, ending, (0, TOK_DEV - HALO, 0)).reshape(MB * TOK_DEV, LATE)
-
     d_gate = d_gate.reshape(MB * TOK_DEV, INNER)
     normed = normed.reshape(MB * TOK_DEV, INNER)
+    late = late.reshape(MB * TOK_DEV, LATE)
     if fits:
         flat = [part.reshape(MB * TOK_DEV, D) for part in (x, cot)]
-        grads = totals(
-            (info, hidden_t, late, d_gate, normed, w_all, w_back, *flat, gain_in, gate_sum.reshape(shard_rows, D))
+        grads, first_sum = totals(
+            (info, hidden_t, late, w_all, d_gate, *flat, w_back, normed, gain_in, first_sum, gate_sum, ending)
             + (d_taps, d_out_gain, d_skip, d_small, sum_f),
             2,
         )
-        return (*grads, turned(first_sum))
+        return (*grads, first_sum)
+
+    ending = (last + shift(before, -1)).astype(BF16)
+    late = lax.dynamic_update_slice(late.reshape(MB, TOK_DEV, LATE), ending, (0, TOK_DEV - HALO, 0)).reshape(MB * TOK_DEV, LATE)
 
     def owned(grad):
         return lax.psum_scatter(grad, "fsdp", scatter_dimension=0, tiled=True)

time: 340 us -> 326 us (0.959); the launches traced: 339 us -> 320 us
  Pallas kernels: 297 us -> 286 us
  local copies, waits for them, and re-layouts: 24.5 us -> 20.2 us
    pallas_call x1, Pallas kernels: 60 us -> 54.3 us  [totals(): pl.pallas_call(partial(total_kernel, levels, columns), in_specs=[SCALARS]...]
    pallas_call x1, Pallas kernels: 50.5 us -> 46.1 us  [on_device(): call(partial(final_kernel, levels if fits else 0), (MB,), [SCALARS, zx_va...]
    concatenate x1, local copies, waits for them, and re-layouts: 0.01 us -> 4.14 us  [on_device(): flat = jnp.concatenate(small)]
    pad x6 -> x0, local copies, waits for them, and re-layouts: 4.01 us -> none  [padded(): jnp.pad(part, ((0, 0),) * (part.ndim - 1) + ((0, width - part.shape[-1]),))]
    unnamed x43 -> x34, local copies, waits for them, and re-layouts: 16.6 us -> 14.6 us
  transfers between devices with their start and end apart: 1 -> 0, of which waited for: 1 -> 0; matrix products, arithmetic and copies ran while one was open for 1% -> 0% of each run, Pallas kernels for 0% -> 0%
where the time goes in v1:
time: 326 us; the launch traced here: 320 us
  Pallas kernels  286 us (88%)
  local copies, waits for them, and re-layouts  20.2 us (6%)
  matrix products  11.1 us (3%)
    pallas_call x1, Pallas kernels, on_device(): call(partial(mixer_kernel, levels, shards // 2), (5 * MB,), [SCALARS, ear...  152 us
    pallas_call x1, Pallas kernels, totals(): pl.pallas_call(partial(total_kernel, levels, columns), in_specs=[SCALARS]...  54.3 us
    pallas_call x1, Pallas kernels, on_device(): call(partial(final_kernel, levels if fits else 0), (MB,), [SCALARS, zx_va...  46.1 us
    pallas_call x1, Pallas kernels, gather_weights(): pl.pallas_call(partial(gather_kernel, count, columns), in_specs=[SCALARS]...  33.6 us
    unnamed x34, local copies, waits for them, and re-layouts  14.6 us
    dot_general x1, matrix products, on_device(): jnp.dot(hidden.reshape(MB * rows, D), w_all, preferred_element_type=F32)  11.1 us

profile of v1, /device:TPU:0, one launch (start us, length us, event | category | flops | bytes accessed | tf_op | source)
XLA Modules:
  0.0 320.3 jit_solution(6515361172228020917)
XLA Ops:
  0.6 0.8 copy.32
  1.4 0.1 reshape_squeeze.9
  1.5 0.6 pad_add_fusion.info
  2.1 0.8 reshape.75
  2.9 4.1 %concatenate.7 = bf16[2680]{0:T(1024)(128)(2,1)S(1)} concatenate(bf16[1664]{0:T(1024)(128)(2,1)S(1)} %reshape.75, bf16[416]{0:T(512)(128)(2,1)} %param.21, bf16[384]{0:T(512)(128)(2,1)} %param.25, bf16[192]{0:T(256)(128)(2,1)} %param.16, bf16[12]{0:T(256)(128)(2,1)} %param.22, bf16[6]{0:T(256)(128)(2,1)} %param.23, bf16[6]{0:T(256)(128)(2,1)} %param.24), dimensions={0} | concatenate | bytes 10720 | tf_op jit(solution)/shard_map/concatenate | solution.py:1642
  7.0 0.6 pad_bitcast_fusion.mine
  7.6 1.5 copy.33.w_step
  9.1 33.6 %shard_map.237 = (bf16[768,3328]{1,0:T(8,128)(2,1)}, bf16[3,264,768]{2,1,0:T(8,128)(2,1)}, bf16[768,768]{1,0:T(8,128)(2,1)}, bf16[3,256,768]{2,1,0:T(8,128)(2,1)...) custom-call(s32[8]{0:T(128)} %pad_add_fusion.info, ...), custom_call_target="tpu_custom_call" | custom-call | tf_op jit(solution)/shard_map/pallas_call | solution.py:330
  42.6 11.1 %fusion.vals.bc_in.dt.gate = f32[3,264,3328]{2,1,0:T(8,128)} fusion(bf16[3,264,768]{2,1,0:T(8,128)(2,1)} %get-tuple-element.71, bf16[768,3328]{1,0:T(8,128)(2,1)} %get-tuple-element.72.w_all_in), kind=kOutput, calls=%fused_computation | convolution fusion | flops 4048551936 | bytes 16871424 | tf_op jit(solution)/shard_map/dot_general | solution.py:1649
  53.7 152.2 %shard_map.238 = (bf16[3,256,1536]{2,1,0:T(8,128)(2,1)}, f32[3,256,128]{2,1,0:T(8,128)}, f32[3,256,128]{2,1,0:T(8,128)}, f32[3,256,128]{2,1,0:T(8,128)}, f32[3,6...) custom-call(s32[8]{0:T(128)} %pad_add_fusion.info, ...), custom_call_target="tpu_custom_call" | custom-call | flops 49999998976 | bytes 60000000 | tf_op jit(solution)/shard_map/pallas_call | solution.py:1683
  205.9 46.1 %shard_map.239 = (bf16[3,256,1792]{2,1,0:T(8,128)(2,1)}, f32[3,8,1664]{2,1,0:T(8,128)}, f32[3,8,1664]{2,1,0:T(8,128)}, f32[3,8,1664]{2,1,0:T(8,128)}, f32[8,1664...) custom-call(s32[8]{0:T(128)} %pad_add_fusion.info, ...), custom_call_target="tpu_custom_call" | custom-call | flops 2000000000 | bytes 40000000 | tf_op jit(solution)/shard_map/pallas_call | solution.py:1741
  252.1 54.3 %shard_map.240 = (bf16[768,768]{1,0:T(8,128)(2,1)}, f32[768,768]{1,0:T(8,128)}, f32[384,768]{1,0:T(8,128)}, f32[192,3072]{1,0:T(8,128)}, f32[192,128]{1,0:T(8,12...) custom-call(s32[8]{0:T(128)} %pad_add_fusion.info, ...), custom_call_target="tpu_custom_call" | custom-call | tf_op jit(solution)/shard_map/pallas_call | solution.py:1593
  306.3 1.3 reduce
  307.6 1.7 copy.36
  309.3 2.4 copy.48
  311.7 0.0 copy-done.1
  311.7 1.4 copy.49
  313.1 0.0 copy-done.6
  313.1 0.6 copy.50
  313.7 0.5 copy-done
  314.2 0.0 copy-start.8
  314.3 0.0 copy-start.7
  314.3 0.0 copy-start.2
  314.3 1.4 copy.51
  315.7 0.6 copy.52
  316.3 0.6 copy.53
  316.9 0.6 copy.54
  317.5 0.5 copy.55
  318.0 0.5 copy.56
  318.5 0.5 copy.57
  319.1 0.0 copy-done.2
  319.1 1.0 copy.58
  (13 shorter events, 0.0 us)
Async XLA Ops:
  307.6 4.1 %copy-start.1 = (f32[768,768]{1,0:T(8,128)S(1)}, f32[768,768]{1,0:T(8,128)}, u32[]{:S(2)}) copy-start(f32[768,768]{1,0:T(8,128)} %get-tuple-element.115) | copy-start | bytes 7077892
  311.7 1.4 copy-start.6
  311.7 2.5 copy-start
  314.2 1.5 copy-start.3
  314.2 2.1 copy-start.4
  314.2 2.7 copy-start.5
  314.2 3.3 %copy-start.9 = (f32[1,12]{1,0:T(1,128)S(1)}, f32[1,12]{1,0:T(1,128)}, u32[]{:S(2)}) copy-start(f32[1,12]{1,0:T(1,128)} %get-tuple-element.122) | copy-start | bytes 148
  314.2 3.8 %copy-start.8 = (f32[1,6]{1,0:T(1,128)S(1)}, f32[1,6]{1,0:T(1,128)}, u32[]{:S(2)}) copy-start(f32[1,6]{1,0:T(1,128)} %get-tuple-element.123) | copy-start | bytes 76
  314.3 4.3 %copy-start.7 = (f32[1,6]{1,0:T(1,128)S(1)}, f32[1,6]{1,0:T(1,128)}, u32[]{:S(2)}) copy-start(f32[1,6]{1,0:T(1,128)} %get-tuple-element.124) | copy-start | bytes 76
  314.3 4.8 %copy-start.2 = (f32[384,768]{1,0:T(8,128)S(1)}, f32[384,768]{1,0:T(8,128)}, u32[]{:S(2)}) copy-start(f32[384,768]{1,0:T(8,128)} %get-tuple-element.178) | copy-start | bytes 3538948

commit v2 on v1

--- a/solution.py
+++ b/solution.py
@@ -129,8 +129,10 @@
 
 
 def gather_kernel(
-    count, columns, info, x_in, cot_in, w_inner, w_state, w_step, mine,
-    w_all, hidden, hidden_t, d_branch, d_branch_t, norm, taps, steps, skip, scale, spread_f, spread_r, sum_f, sum_r,
+    count, columns, info, x_hbm, cot_hbm, w_inner, w_state, w_step, mine,
+    w_all_out, hidden_out, hidden_t_out, d_branch_out, d_branch_t_out, spread_f_out, spread_r_out, sum_f_out, sum_r_out,
+    norm, taps, steps, skip, scale,
+    x_in, cot_in, w_all, hidden, hidden_t, d_branch, d_branch_t, spread_f, spread_r, sum_f, sum_r, load_sems, keep_sems, row_sems,
     halo, small, skip_row, halo_sems, small_sems, x_sems, y_sems, mate_sems, own_sems,
 ):
     me, part = lax.axis_index("dp"), lax.axis_index("fsdp")
@@ -140,6 +142,25 @@
     shards = 2 * columns
     rows = w_inner.shape[0]
     chunk = rows // (2 * CUTS)
+    here = pl.ds(pl.multiple_of(part * rows, 16), rows)
+    results = (
+        (hidden, hidden_out), (hidden_t, hidden_t_out), (d_branch, d_branch_out), (d_branch_t, d_branch_t_out),
+        (spread_f, spread_f_out), (spread_r, spread_r_out), (sum_f, sum_f_out), (sum_r, sum_r_out),
+    )
+
+    def load(i):
+        source = (w_inner, x_hbm, cot_hbm)[i]
+        return pltpu.make_async_copy(source, (w_all.at[here, : 2 * INNER], x_in, cot_in)[i], load_sems.at[i])
+
+    def keep(i):
+        return pltpu.make_async_copy(*results[i], keep_sems.at[i])
+
+    def keep_rows(owner):
+        at = pl.ds(pl.multiple_of(owner * rows, 16), rows)
+        return pltpu.make_async_copy(w_all.at[at], w_all_out.at[at], row_sems.at[owner])
+
+    for i in range(3):
+        load(i).start()
 
     barrier = pltpu.get_barrier_semaphore()
 
@@ -194,22 +215,24 @@
         at = w_all.at[pl.ds(pl.multiple_of(owner * rows, 16), rows)]
         return remote(at, at, own_sems, 0, {"fsdp": mate})
 
-    @pl.when(has_next)
-    def _():
-        edge.start()
-
     for d in range(1, shards):
         small_copy(d, False).start()
-    here = pl.ds(pl.multiple_of(part * rows, 16), rows)
-    w_all[here, : 2 * INNER] = w_inner[...]
     w_all[here, 2 * INNER : 2 * INNER + 2 * STATE] = w_state[...]
     w_all[here, 2 * INNER + 2 * STATE :] = jnp.concatenate(
         [w_step[...].astype(F32), jnp.zeros((rows, LANES - 2 * HEADS), F32)], axis=1
     ).astype(BF16)
+    load(0).wait()
     for k in range(2):
         for d in range(1, columns):
             x_copy(k, d).start()
     own_copy(part).start()
+    keep_rows(part).start()
+    load(1).wait()
+    load(2).wait()
+
+    @pl.when(has_next)
+    def _():
+        edge.start()
 
     @pl.when(me == 0)
     def _():
@@ -231,6 +254,8 @@
         value = jnp.where(valid > 0.0, cot_in[m].astype(F32), 0.0)
         d_branch[m] = value.astype(BF16)
         d_branch_t[:, m * TOK_DEV : (m + 1) * TOK_DEV] = jnp.transpose(value).astype(BF16)
+    for i in range(2, 8):
+        keep(i).start()
 
     for ref in (norm, taps, steps, skip_row):
         ref[...] = jnp.zeros_like(ref)
@@ -304,8 +329,13 @@
             pass_on(k - 1)
     for m in range(CUTS, MB):
         hide(m)
+    keep(0).start()
+    keep(1).start()
+    own_copy(mate).wait_recv()
+    keep_rows(mate).start()
     pass_on(CUTS - 1)
-    own_copy(mate).wait_recv()
+    for d in range(1, columns):
+        keep_rows(2 * column_at(d) + core).start()
     own_copy(part).wait_send()
     for k in range(CUTS):
         for d in range(1, columns):
@@ -314,8 +344,14 @@
                 mate_copy(k, d, half, False).wait_send()
             x_copy(k, d).wait_send()
             y_copy(k, d, False).wait_send()
+    for d in range(1, columns):
+        keep_rows(2 * column_at(d) + 1 - core).start()
     for d in range(1, shards):
         small_copy(d, False).wait_send()
+    for owner in range(shards):
+        keep_rows(owner).wait()
+    for i in range(8):
+        keep(i).wait()
 
     @pl.when(has_next)
     def _():
@@ -327,23 +363,30 @@
     columns = shards // 2
     whole = pl.BlockSpec(memory_space=pltpu.VMEM)
     pairs = CUTS * columns
-    return pl.pallas_call(
+    anywhere = pl.BlockSpec(memory_space=pl.ANY)
+    results = [
+        struct(D, WIDE, dtype=BF16), struct(MB, TOK_DEV + HALO, D, dtype=BF16), struct(D, MB * TOK_DEV, dtype=BF16),
+        struct(MB, TOK_DEV, D, dtype=BF16), struct(D, MB * TOK_DEV, dtype=BF16),
+        struct(2 * LANES, INNER, dtype=BF16), struct(2 * LANES, INNER, dtype=BF16),
+        struct(INNER, LANES, dtype=BF16), struct(INNER, LANES, dtype=BF16),
+    ]
+    rows = pltpu.VMEM((MB, TOK_DEV, D), BF16)
+    outs = pl.pallas_call(
         partial(gather_kernel, count, columns),
-        in_specs=[SCALARS] + [whole] * 6,
-        out_specs=[whole] * 14,
-        out_shape=[
-            struct(D, WIDE, dtype=BF16), struct(MB, TOK_DEV + HALO, D, dtype=BF16), struct(D, MB * TOK_DEV, dtype=BF16),
-            struct(MB, TOK_DEV, D, dtype=BF16), struct(D, MB * TOK_DEV, dtype=BF16), struct(1, D), struct(8, CONV_COLS), struct(8, LANES), struct(8, INNER), struct(8, INNER),
-            struct(2 * LANES, INNER, dtype=BF16), struct(2 * LANES, INNER, dtype=BF16),
-            struct(INNER, LANES, dtype=BF16), struct(INNER, LANES, dtype=BF16),
-        ],
-        scratch_shapes=[
+        in_specs=[SCALARS, anywhere, anywhere, anywhere, whole, whole, whole],
+        out_specs=[anywhere] * 9 + [whole] * 5,
+        out_shape=results + [struct(1, D), struct(8, CONV_COLS), struct(8, LANES), struct(8, INNER), struct(8, INNER)],
+        scratch_shapes=[rows, rows]
+        + [pltpu.VMEM(result.shape, result.dtype) for result in results]
+        + [pltpu.SemaphoreType.DMA((3,)), pltpu.SemaphoreType.DMA((8,)), pltpu.SemaphoreType.DMA((shards,))]
+        + [
             pltpu.VMEM((MB, 2 * HALO, D), BF16), pltpu.VMEM((shards,) + mine.shape, BF16), pltpu.VMEM((8, LANES), F32),
             pltpu.SemaphoreType.DMA((2, 1)), pltpu.SemaphoreType.DMA((2, shards)), pltpu.SemaphoreType.DMA((2, pairs)),
             pltpu.SemaphoreType.DMA((2, pairs)), pltpu.SemaphoreType.DMA((2, 2 * pairs)), pltpu.SemaphoreType.DMA((2, 1)),
         ],
         compiler_params=pltpu.CompilerParams(vmem_limit_bytes=VMEM_LIMIT, collective_id=identity, has_side_effects=True),
     )(info, x, cot, w_inner, w_state, w_step, mine)
+    return outs[:5] + outs[9:] + outs[5:9]
 
 
 def front_body(m, info, vals, bc, dt, taps, steps, spread_f, spread_r, v_out, bc_out, fr_out, frp_out, tot_f, tot_r, kept_f, kept_r, dx_out):

time: 326 us -> 322 us (0.988)
  Pallas kernels: 286 us -> 282 us
    pallas_call x1, Pallas kernels: 33.6 us -> 29.8 us  [gather_weights(): pl.pallas_call(partial(gather_kernel, count, columns), in_specs=[SCALARS,...]
where the time goes in v2:
time: 322 us; the launch traced here: 316 us
  Pallas kernels  282 us (88%)
  local copies, waits for them, and re-layouts  20.2 us (6%)
  matrix products  11.1 us (3%)
    pallas_call x1, Pallas kernels, on_device(): call(partial(mixer_kernel, levels, shards // 2), (5 * MB,), [SCALARS, ear...  152 us
    pallas_call x1, Pallas kernels, totals(): pl.pallas_call(partial(total_kernel, levels, columns), in_specs=[SCALARS]...  54.2 us
    pallas_call x1, Pallas kernels, on_device(): call(partial(final_kernel, levels if fits else 0), (MB,), [SCALARS, zx_va...  46.3 us
    pallas_call x1, Pallas kernels, gather_weights(): pl.pallas_call(partial(gather_kernel, count, columns), in_specs=[SCALARS,...  29.8 us
    unnamed x34, local copies, waits for them, and re-layouts  14.6 us
    dot_general x1, matrix products, on_device(): jnp.dot(hidden.reshape(MB * rows, D), w_all, preferred_element_type=F32)  11.1 us

profile of v2, /device:TPU:0, one launch (start us, length us, event | category | flops | bytes accessed | tf_op | source)
XLA Modules:
  0.0 316.5 jit_solution(15404178061279205989)
XLA Ops:
  0.6 0.8 copy.32
  1.4 0.1 reshape_squeeze.9
  1.5 0.6 pad_add_fusion.info
  2.1 0.8 reshape.75
  2.9 4.1 %concatenate.7 = bf16[2680]{0:T(1024)(128)(2,1)S(1)} concatenate(bf16[1664]{0:T(1024)(128)(2,1)S(1)} %reshape.75, bf16[416]{0:T(512)(128)(2,1)} %param.21, bf16[384]{0:T(512)(128)(2,1)} %param.25, bf16[192]{0:T(256)(128)(2,1)} %param.16, bf16[12]{0:T(256)(128)(2,1)} %param.22, bf16[6]{0:T(256)(128)(2,1)} %param.23, bf16[6]{0:T(256)(128)(2,1)} %param.24), dimensions={0} | concatenate | bytes 10720 | tf_op jit(solution)/shard_map/concatenate | solution.py:1685
  7.0 0.6 pad_bitcast_fusion.mine
  7.6 1.5 copy.33.w_step
  9.1 29.8 %shard_map.237 = (bf16[768,3328]{1,0:T(8,128)(2,1)}, bf16[3,264,768]{2,1,0:T(8,128)(2,1)}, bf16[768,768]{1,0:T(8,128)(2,1)}, bf16[3,256,768]{2,1,0:T(8,128)(2,1)...) custom-call(s32[8]{0:T(128)} %pad_add_fusion.info, ...), custom_call_target="tpu_custom_call" | custom-call | tf_op jit(solution)/shard_map/pallas_call | solution.py:374
  38.9 11.1 %fusion.vals.bc_in.dt.gate = f32[3,264,3328]{2,1,0:T(8,128)} fusion(bf16[3,264,768]{2,1,0:T(8,128)(2,1)} %get-tuple-element.71, bf16[768,3328]{1,0:T(8,128)(2,1)} %get-tuple-element.72.w_all_in), kind=kOutput, calls=%fused_computation | convolution fusion | flops 4048551936 | bytes 16871424 | tf_op jit(solution)/shard_map/dot_general | solution.py:1692
  50.0 152.1 %shard_map.238 = (bf16[3,256,1536]{2,1,0:T(8,128)(2,1)}, f32[3,256,128]{2,1,0:T(8,128)}, f32[3,256,128]{2,1,0:T(8,128)}, f32[3,256,128]{2,1,0:T(8,128)}, f32[3,6...) custom-call(s32[8]{0:T(128)} %pad_add_fusion.info, ...), custom_call_target="tpu_custom_call" | custom-call | flops 49999998976 | bytes 60000000 | tf_op jit(solution)/shard_map/pallas_call | solution.py:1726
  202.1 46.3 %shard_map.239 = (bf16[3,256,1792]{2,1,0:T(8,128)(2,1)}, f32[3,8,1664]{2,1,0:T(8,128)}, f32[3,8,1664]{2,1,0:T(8,128)}, f32[3,8,1664]{2,1,0:T(8,128)}, f32[8,1664...) custom-call(s32[8]{0:T(128)} %pad_add_fusion.info, ...), custom_call_target="tpu_custom_call" | custom-call | flops 2000000000 | bytes 40000000 | tf_op jit(solution)/shard_map/pallas_call | solution.py:1784
  248.4 54.2 %shard_map.240 = (bf16[768,768]{1,0:T(8,128)(2,1)}, f32[768,768]{1,0:T(8,128)}, f32[384,768]{1,0:T(8,128)}, f32[192,3072]{1,0:T(8,128)}, f32[192,128]{1,0:T(8,12...) custom-call(s32[8]{0:T(128)} %pad_add_fusion.info, ...), custom_call_target="tpu_custom_call" | custom-call | tf_op jit(solution)/shard_map/pallas_call | solution.py:1636
  302.5 1.3 reduce
  303.8 1.7 copy.36
  305.6 2.4 copy.48
  307.9 0.0 copy-done.1
  307.9 1.4 copy.49
  309.3 0.6 copy.50
  309.9 0.5 copy-done
  310.5 0.0 copy-start.8
  310.5 0.0 copy-start.7
  310.5 0.0 copy-start.2
  310.5 1.4 copy.51
  311.9 0.0 copy-done.3
  311.9 0.6 copy.52
  312.5 0.6 copy.53
  313.1 0.6 copy.54
  313.7 0.5 copy.55
  314.2 0.5 copy.56
  314.8 0.5 copy.57
  315.3 0.0 copy-done.2
  315.3 1.0 copy.58
  (13 shorter events, 0.0 us)
Async XLA Ops:
  303.8 4.1 %copy-start.1 = (f32[768,768]{1,0:T(8,128)S(1)}, f32[768,768]{1,0:T(8,128)}, u32[]{:S(2)}) copy-start(f32[768,768]{1,0:T(8,128)} %get-tuple-element.115) | copy-start | bytes 7077892
  307.9 1.4 copy-start.6
  307.9 2.5 copy-start
  310.4 1.5 copy-start.3
  310.4 2.1 copy-start.4
  310.4 2.7 copy-start.5
  310.5 3.3 %copy-start.9 = (f32[1,12]{1,0:T(1,128)S(1)}, f32[1,12]{1,0:T(1,128)}, u32[]{:S(2)}) copy-start(f32[1,12]{1,0:T(1,128)} %get-tuple-element.122) | copy-start | bytes 148
  310.5 3.8 %copy-start.8 = (f32[1,6]{1,0:T(1,128)S(1)}, f32[1,6]{1,0:T(1,128)}, u32[]{:S(2)}) copy-start(f32[1,6]{1,0:T(1,128)} %get-tuple-element.123) | copy-start | bytes 76
  310.5 4.3 %copy-start.7 = (f32[1,6]{1,0:T(1,128)S(1)}, f32[1,6]{1,0:T(1,128)}, u32[]{:S(2)}) copy-start(f32[1,6]{1,0:T(1,128)} %get-tuple-element.124) | copy-start | bytes 76
  310.5 4.8 %copy-start.2 = (f32[384,768]{1,0:T(8,128)S(1)}, f32[384,768]{1,0:T(8,128)}, u32[]{:S(2)}) copy-start(f32[384,768]{1,0:T(8,128)} %get-tuple-element.178) | copy-start | bytes 3538948
